TPU v7x, 256 devices: a whole 4x4x8 slice. The times are simulated.
256 devices in a mesh: dp: 16 (over y, x), expert: 16 (over z, core).
Axes of the slice: x: 4, y: 4, z: 8, core: 2. Of those that a mesh axis runs over, the one named last changes fastest.
Arguments:
- tokens: float32 [2048, 2048], P('expert'), may hold values from -6 to 6
- expert_ids: int32 [2048, 8], P('expert'), may hold values from 0 to 127, all different within a row; in each aligned block of 128 rows (0 to 127, 128 to 255, ...) at most 10 rows name the same one
- gate_values: float32 [2048, 8], P('expert'), may hold values from 0.05 to 1
- valid_mask: int32 [2048], P('expert'), may hold values from 0 to 1, as said below
- gate_weight: bfloat16 [128, 1536, 2048], P('expert', 'dp'), may hold values from -0.125 to 0.125
- up_weight: bfloat16 [128, 1536, 2048], P('expert', 'dp'), may hold values from -0.125 to 0.125
- down_weight: bfloat16 [128, 1536, 2048], P('expert', 'dp'), may hold values from -0.15625 to 0.15625
Outputs:
- blended: float32 [2048, 2048], P('expert')
- loss: float32 [], replicated
Inputs may be any that keep to these rules, and one draw needn't show every extreme that they name: `expert_ids`: each row names 8 different experts; in the 128 rows of one block no expert is named more than 10 times. `valid_mask`: each block of 128 tokens holds at least one valid token.
All inputs are finite; a program needn't handle non-finite values.
Results may differ from a plain program's by a relative error of at most 0.0058.
Values may be sent and summed in bfloat16 or wider, within the bound.
A program may use at most 128 MiB of HBM per device.

v0:
```python
import jax
import jax.numpy as jnp
from jax import lax
from jax.sharding import PartitionSpec as P


def slot_ranks(flattened, expert_total):
    one_hot = (
        flattened[:, :, None] == jnp.arange(expert_total, dtype=jnp.int32)[None, None, :]
    ).astype(jnp.int32)
    before = jnp.cumsum(one_hot, axis=1) - one_hot
    return jnp.sum(before * one_hot, axis=2)


def combine_rows(returned, slot_place, gate_values, weights, tok_count, top_count):
    width = returned.shape[-1]
    flat_rows = returned.reshape(-1, width)
    picked = flat_rows[slot_place].reshape(tok_count, top_count, width)
    return jnp.sum(gate_values[:, :, None] * picked.astype(jnp.float32), axis=1) * weights[:, None]


def on_device(tokens, expert_ids, gate_values, valid_mask, gate_weight, up_weight, down_weight):
    tok_count, model_width = tokens.shape
    top_count = expert_ids.shape[1]
    local_experts = gate_weight.shape[0]
    expert_groups = lax.axis_size("expert")
    expert_total = local_experts * expert_groups
    capacity = max(2, (5 * tok_count * top_count + 4 * expert_total - 1) // (4 * expert_total))
    weights = valid_mask.astype(jnp.float32)
    flattened = expert_ids.reshape(1, tok_count * top_count)
    slot_rank = slot_ranks(flattened, expert_total)
    slot_place = (flattened * capacity + slot_rank).reshape(-1)
    token_rows = jnp.repeat(tokens.astype(jnp.bfloat16), top_count, axis=0)
    outgoing = (
        jnp.zeros((expert_total * capacity, model_width), jnp.bfloat16)
        .at[slot_place]
        .set(token_rows)
    )
    outgoing = outgoing.reshape(expert_groups, local_experts, capacity, model_width)
    arrived = lax.all_to_all(outgoing, "expert", split_axis=0, concat_axis=0, tiled=True)
    gate_pre = jnp.einsum(
        "gecd,efd->gecf", arrived, gate_weight, preferred_element_type=jnp.float32
    )
    up_pre = jnp.einsum("gecd,efd->gecf", arrived, up_weight, preferred_element_type=jnp.float32)
    hidden = (jax.nn.silu(gate_pre) * up_pre).astype(jnp.bfloat16)
    partial_out = jnp.einsum(
        "gecf,efd->gecd", hidden, down_weight, preferred_element_type=jnp.float32
    )
    summed = lax.psum_scatter(partial_out, "dp", scatter_dimension=3, tiled=True).astype(
        jnp.bfloat16
    )
    outputs = lax.all_gather(summed, "dp", axis=3, tiled=True)
    returned = lax.all_to_all(outputs, "expert", split_axis=0, concat_axis=0, tiled=True)
    blended = combine_rows(returned, slot_place, gate_values, weights, tok_count, top_count)
    per_token = jnp.mean(blended * blended, axis=1)
    local_loss = jnp.sum(per_token * weights)
    loss_sum, token_total = lax.psum((local_loss, jnp.sum(weights)), "expert")
    return (blended, loss_sum / token_total)


def solution(mesh):
    return jax.shard_map(
        on_device,
        mesh=mesh,
        in_specs=(
            P("expert", None),
            P("expert", None),
            P("expert", None),
            P("expert"),
            P("expert", "dp", None),
            P("expert", "dp", None),
            P("expert", "dp", None),
        ),
        out_specs=(P("expert", None), P()),
        check_vma=False,
    )
```

profile of v0, /device:TPU:32, one launch (start us, length us, event | category | flops | bytes accessed | tf_op | source)
XLA Modules:
  0.0 545.6 jit_solution(17804552983776204372)
XLA Ops:
  7.2 0.0 copy-start
  7.2 0.0 reduce-scatter.2.cloned.1.call-start
  7.2 0.9 copy.38
  8.2 0.1 eq.27
  8.3 0.2 fusion.20
  8.5 0.3 fusion.18
  8.8 0.9 copy.40
  9.7 0.7 broadcast_multiply_fusion.1
  10.4 0.1 copy.37
  10.5 0.1 mul.54
  10.6 2.1 convert_element_type.30
  12.7 1.4 fusion.17
  14.1 10.1 %scatter_custom_fusion = bf16[1280,2048]{1,0:T(8,128)(2,1)} fusion(s32[1024]{0:T(1024)S(1)} %bitcast.61, bf16[]{:T(256)} %constant.7.clone.1, bf16[128,2048]{1,0:T(8,128)(2,1)} %convert_element_type.30), kind=kCustom, calls=%fused_computation.9 | custom fusion | bytes 5767170 | tf_op jit(solution)/shard_map/scatter | solution.py:37
  24.3 9.5 %reshape.177 = bf16[16,8,10,2048]{3,2,1,0:T(8,128)(2,1)} reshape(bf16[1280,2048]{1,0:T(8,128)(2,1)} %scatter_custom_fusion) | data formatting | bytes 10485760 | tf_op jit(solution)/shard_map/reshape | solution.py:39
  33.8 6.8 %copy.41 = bf16[16,8,10,2048]{3,1,2,0:T(8,128)(2,1)S(1)} copy(bf16[16,8,10,2048]{3,2,1,0:T(8,128)(2,1)} %reshape.177) | data formatting | bytes 10485760 | tf_op jit(solution)/shard_map/reshape | solution.py:39
  40.6 0.0 copy-start.4
  40.6 124.0 %all_to_all.10 = bf16[16,8,10,2048]{3,1,2,0:T(8,128)(2,1)S(1)} all-to-all(bf16[16,8,10,2048]{3,1,2,0:T(8,128)(2,1)S(1)} %copy.41), channel_id=1, replica_groups=mesh['dp'=16,'expert'=16] {'expert'}, dimensions={0} | all-to-all | bytes 10485760 | tf_op jit(solution)/shard_map/all_to_all | solution.py:40
  164.6 0.0 copy-done.4
  164.6 0.0 copy-start.5
  164.6 3.2 fusion.1
  167.9 0.0 copy-done.5
  167.9 3.2 fusion.3
  171.1 0.8 fusion.12
  171.9 0.0 copy-done
  171.9 5.5 %convolution_bitcast_fusion = f32[16,8,10,2048]{3,0,2,1:T(8,128)} fusion(bf16[8,96,2048]{2,1,0:T(8,128)(2,1)S(1)} %copy-done, bf16[16,8,10,96]{3,1,2,0:T(8,128)(2,1)S(1)} %fusion.12), kind=kOutput, calls=%fused_computation.4 | convolution fusion | flops 503316480 | bytes 13877248 | tf_op jit(solution)/shard_map/gecf,efd->gecd/dot_general | solution.py:46
  177.4 0.0 reduce-scatter.2.cloned.1.call-update
  177.5 0.0 all-gather.2.cloned.1.call-start
  177.5 95.5 %reduce-scatter.2.cloned.1.call-done = f32[16,8,10,128]{3,0,2,1:T(8,128)} async-done(((f32[16,8,10,2048]{3,0,2,1:T(8,128)}), f32[16,8,10,128]{3,0,2,1:T(8,128)}) %reduce-scatter.2.cloned.1.call-update) | async-done | bytes 655376 | tf_op jit(solution)/shard_map/reduce_scatter | solution.py:49
  273.0 1.9 convert_element_type.32
  274.8 0.0 all-gather.2.cloned.1.call-update
  274.9 67.3 %all-gather.2.cloned.1.call-done = bf16[16,8,10,2048]{3,0,2,1:T(8,128)(2,1)} async-done(((bf16[16,8,10,128]{3,0,2,1:T(8,128)(2,1)}), bf16[16,8,10,2048]{3,0,2,1:T(8,128)(2,1)}) %all-gather.2.cloned.1.call-update) | async-done | bytes 5242896 | tf_op jit(solution)/shard_map/all_gather | solution.py:52
  342.2 7.7 %copy.47 = bf16[16,8,10,2048]{3,1,2,0:T(8,128)(2,1)} copy(bf16[16,8,10,2048]{3,0,2,1:T(8,128)(2,1)} %all-gather.2.cloned.1.call-done) | data formatting | bytes 10485760 | tf_op jit(solution)/shard_map/all_gather | solution.py:52
  349.8 0.0 copy-start.2
  349.8 0.0 copy-start.3
  349.8 7.6 %all-to-all-start.1 = ((bf16[16,8,10,2048]{3,1,2,0:T(8,128)(2,1)}), bf16[16,8,10,2048]{3,1,2,0:T(8,128)(2,1)}, u32[]{:S(2)}, u32[]{:S(2)}) async-start(bf16[16,8,10,2048]{3,1,2,0:T(8,128)(2,1)} %copy.47), calls=%async_computation.2 | async-start | bytes 10485760 | tf_op jit(solution)/shard_map/all_to_all | solution.py:53
  357.5 0.0 copy-done.2
  357.5 0.1 copy.36
  357.6 0.0 copy-done.3
  357.6 114.7 %all-to-all-done.1 = bf16[16,8,10,2048]{3,1,2,0:T(8,128)(2,1)} async-done(((bf16[16,8,10,2048]{3,1,2,0:T(8,128)(2,1)}), bf16[16,8,10,2048]{3,1,2,0:T(8,128)(2,1)}, u32[]{:S(2)}, u32[]{:S(2)}) %all-to-all-start.1) | async-done | bytes 5242912 | tf_op jit(solution)/shard_map/all_to_all | solution.py:53
  472.3 10.4 %copy.48 = bf16[16,8,10,2048]{3,2,1,0:T(8,128)(2,1)} copy(bf16[16,8,10,2048]{3,1,2,0:T(8,128)(2,1)} %all-to-all-done.1) | data formatting | bytes 10485760 | tf_op jit(solution)/shard_map/all_to_all | solution.py:53
  482.7 9.8 %reshape.178 = bf16[1280,2048]{1,0:T(8,128)(2,1)} reshape(bf16[16,8,10,2048]{3,2,1,0:T(8,128)(2,1)} %copy.48) | data formatting | bytes 10485760 | tf_op jit(solution)/shard_map/reshape | solution.py:17
  492.5 0.0 copy-start.1
  492.5 12.1 %gather_fusion = bf16[1024,2048]{1,0:T(8,128)(2,1)} fusion(bf16[1280,2048]{1,0:T(8,128)(2,1)} %reshape.178, s32[1024]{0:T(1024)S(1)} %broadcast_clamp_fusion), kind=kCustom, calls=%fused_computation | custom fusion | bytes 8392704 | tf_op jit(solution)/shard_map/gather | solution.py:18
  504.6 6.5 %fusion = f32[128,2048]{1,0:T(8,128)S(1)} fusion(bf16[1024,2048]{1,0:T(8,128)(2,1)} %gather_fusion, f32[128,8]{1,0:T(8,128)S(1)} %copy.36), kind=kLoop, calls=%fused_computation.3 | loop fusion | flops 6029312 | bytes 5246976 | tf_op jit(solution)/shard_map/reduce_sum | solution.py:19
  511.2 1.1 multiply_reduce_fusion
  512.3 0.7 convert_reduce_fusion
  513.0 23.4 %all-reduce = (f32[]{:T(128)}, f32[]{:T(128)}) all-reduce(f32[]{:T(128)} %get-tuple-element.3, f32[]{:T(128)} %get-tuple-element.2), channel_id=1, replica_groups=mesh['dp'=16,'expert'=16] {'expert'}, use_global_device_ids=true, to_apply=%region_8.9 | all-reduce | flops 2 | bytes 16 | tf_op jit(solution)/shard_map/psum | solution.py:57
  537.6 0.0 copy-done.1
  (7 shorter events, 0.1 us)
Async XLA Ops:
  7.2 164.8 %copy-start = (bf16[8,96,2048]{2,1,0:T(8,128)(2,1)S(1)}, bf16[8,96,2048]{2,1,0:T(8,128)(2,1)}, u32[]{:S(2)}) copy-start(bf16[8,96,2048]{2,1,0:T(8,128)(2,1)} %param.13) | copy-start | bytes 9437188
  7.2 265.8 %reduce-scatter.2.cloned.1.call-start = ((), (), s32[]{:S(2)}) async-start(), calls=%async_computation.3 | async-start | bytes 11141120 | tf_op jit(solution)/shard_map/reduce_scatter | solution.py:49
  40.6 124.0 %copy-start.4 = (bf16[8,96,2048]{2,1,0:T(8,128)(2,1)S(1)}, bf16[8,96,2048]{2,1,0:T(8,128)(2,1)}, u32[]{:S(2)}) copy-start(bf16[8,96,2048]{2,1,0:T(8,128)(2,1)} %param.12) | copy-start | bytes 9437188
  164.6 3.2 copy-start.5
  177.5 164.7 %all-gather.2.cloned.1.call-start = ((), (), s32[]{:S(2)}) async-start(), calls=%async_computation.4 | async-start | bytes 5570560 | tf_op jit(solution)/shard_map/all_gather | solution.py:52
  349.8 7.6 %copy-start.2 = (f32[128,8]{0,1:T(8,128)S(1)}, f32[128,8]{0,1:T(8,128)}, u32[]{:S(2)}) copy-start(f32[128,8]{0,1:T(8,128)} %param.9) | copy-start | bytes 12292
  349.8 7.7 %copy-start.3 = (s32[128]{0:T(128)S(1)}, s32[128]{0:T(128)}, u32[]{:S(2)}) copy-start(s32[128]{0:T(128)} %param.10) | copy-start | bytes 1540
  349.8 122.5 %all-to-all-start.1 = ((bf16[16,8,10,2048]{3,1,2,0:T(8,128)(2,1)}), bf16[16,8,10,2048]{3,1,2,0:T(8,128)(2,1)}, u32[]{:S(2)}, u32[]{:S(2)}) async-start(bf16[16,8,10,2048]{3,1,2,0:T(8,128)(2,1)} %copy.47), calls=%async_computation.2 | async-start | bytes 10485760 | tf_op jit(solution)/shard_map/all_to_all | solution.py:53
  492.5 45.1 %copy-start.1 = (bf16[8,96,2048]{2,1,0:T(8,128)(2,1)S(1)}, bf16[8,96,2048]{2,1,0:T(8,128)(2,1)}, u32[]{:S(2)}) copy-start(bf16[8,96,2048]{2,1,0:T(8,128)(2,1)} %param.13) | copy-start | bytes 9437188
Sparse Core Ops, SparseCore 0:
  177.6 95.3 reduce-scatter.1
  276.0 66.1 all-gather.1
where the time goes:
time: 550 us; the launch traced here: 546 us
  waiting for transfers between devices  278 us (51%)
  blocking collectives  147 us (27%)
  local copies, waits for them, and re-layouts  68.8 us (13%)
  between operations  16.5 us (3%)
  other arithmetic  15.7 us (3%)
  matrix products  12 us (2%)
  starting transfers between devices  7.71 us (1%)
    all_to_all x1, blocking collectives, on_device(): lax.all_to_all(outgoing, 'expert', split_axis=0, concat_axis=0, tiled=True)  124 us
    all_to_all x1, waiting for transfers between devices, on_device(): lax.all_to_all(outputs, 'expert', split_axis=0, concat_axis=0, tiled=True)  115 us
    reduce_scatter x1, waiting for transfers between devices, on_device(): lax.psum_scatter(partial_out, 'dp', scatter_dimension=3, tiled=True)  95.5 us
    all_gather x1, waiting for transfers between devices, on_device(): outputs = lax.all_gather(summed, 'dp', axis=3, tiled=True)  67.3 us
    psum x1, blocking collectives, on_device(): loss_sum, token_total = lax.psum((local_loss, jnp.sum(weights)), 'expert')  23.4 us
    reshape x2, local copies, waits for them, and re-layouts, on_device(): outgoing.reshape(expert_groups, local_experts, capacity, model_width)  16.3 us
    gather x1, local copies, waits for them, and re-layouts, combine_rows(): picked = flat_rows[slot_place].reshape(tok_count, top_count, width)  12.1 us
  transfers between devices with their start and end apart: 3, of which 3 were waited for; matrix products, arithmetic and copies ran while one was open for 0% of the time, Pallas kernels for 0%

commit v1 on v0

v1 whole, which is shorter than its diff:
```python
import jax
import jax.numpy as jnp
from jax import lax
from jax.sharding import PartitionSpec as P

SLOTS = 16


def on_device(tokens, expert_ids, gate_values, valid_mask, gate_weight, up_weight, down_weight):
    tok_count, width = tokens.shape
    local_experts = gate_weight.shape[0]
    blocks = lax.axis_size("expert")
    parts = lax.axis_size("dp")
    piece = width // parts
    me = lax.axis_index("expert")
    part = lax.axis_index("dp")
    weights = valid_mask.astype(jnp.float32)
    mine = lax.dynamic_slice(tokens, (0, part * piece), (tok_count, piece)).astype(jnp.bfloat16)
    column = lax.all_gather(mine, "expert", axis=0, tiled=True)
    every = lax.all_gather(column, "dp", axis=1, tiled=True)
    ids = lax.all_gather(expert_ids, "expert", axis=0, tiled=True)
    gates = lax.all_gather(gate_values * weights[:, None], "expert", axis=0, tiled=True)
    local = me * local_experts + jnp.arange(local_experts, dtype=jnp.int32)
    match = ids[:, None, :] == local[None, :, None]
    named = jnp.any(match, axis=2)
    gate = jnp.sum(jnp.where(match, gates[:, None, :], 0.0), axis=2).reshape(blocks, tok_count, local_experts)
    taken = named.astype(jnp.int32).reshape(blocks, tok_count, local_experts)
    rank = jnp.cumsum(taken, axis=1) - taken
    pick = (
        (rank.transpose(0, 2, 1)[:, :, None, :] == jnp.arange(SLOTS, dtype=jnp.int32)[None, None, :, None])
        & (taken.transpose(0, 2, 1)[:, :, None, :] > 0)
    )
    slot_gate = jnp.sum(jnp.where(pick, gate.transpose(0, 2, 1)[:, :, None, :], 0.0), axis=3)
    pick = pick.astype(jnp.bfloat16)
    rows = jnp.einsum(
        "best,btf->ebsf", pick, every.reshape(blocks, tok_count, width), preferred_element_type=jnp.float32
    ).astype(jnp.bfloat16)
    rows = rows.reshape(local_experts, blocks * SLOTS, width)
    gate_pre = jnp.einsum("erd,efd->erf", rows, gate_weight, preferred_element_type=jnp.float32)
    up_pre = jnp.einsum("erd,efd->erf", rows, up_weight, preferred_element_type=jnp.float32)
    hidden = (jax.nn.silu(gate_pre) * up_pre).astype(jnp.bfloat16)
    out = jnp.einsum("erf,efd->erd", hidden, down_weight, preferred_element_type=jnp.float32)
    out = out.reshape(local_experts, blocks, SLOTS, width) * slot_gate.transpose(1, 0, 2)[:, :, :, None]
    mixed = jnp.einsum(
        "best,ebsf->btf", pick, out.astype(jnp.bfloat16), preferred_element_type=jnp.float32
    ).reshape(blocks * tok_count, width)
    summed = lax.psum_scatter(mixed.astype(jnp.bfloat16), "dp", scatter_dimension=1, tiled=True)
    own = lax.psum_scatter(summed.astype(jnp.float32), "expert", scatter_dimension=0, tiled=True)
    blended = lax.all_gather(own, "dp", axis=1, tiled=True)
    per_token = jnp.mean(blended * blended, axis=1)
    local_loss = jnp.sum(per_token * weights)
    loss_sum, token_total = lax.psum((local_loss, jnp.sum(weights)), "expert")
    return (blended, loss_sum / token_total)


def solution(mesh):
    return jax.shard_map(
        on_device,
        mesh=mesh,
        in_specs=(
            P("expert", None),
            P("expert", None),
            P("expert", None),
            P("expert"),
            P("expert", "dp", None),
            P("expert", "dp", None),
            P("expert", "dp", None),
        ),
        out_specs=(P("expert", None), P()),
        check_vma=False,
    )
```

time: 550 us -> 416 us (0.76)
  blocking collectives: 147 us -> 74.3 us
  local copies, waits for them, and re-layouts: 68.8 us -> 29.2 us
  waiting for transfers between devices: 278 us -> 240 us
  matrix products: 12 us -> 42.7 us
  starting transfers between devices: 7.71 us -> 0.16 us
  other arithmetic: 15.7 us -> 9.1 us
    all_to_all x1 -> x0, blocking collectives: 124 us -> none  [on_device(): lax.all_to_all(outgoing, 'expert', split_axis=0, concat_axis=0, tiled=True)]
    all_to_all x1 -> x0, waiting for transfers between devices: 115 us -> none  [on_device(): lax.all_to_all(outputs, 'expert', split_axis=0, concat_axis=0, tiled=True)]
    unnamed x2 -> x5, waiting for transfers between devices: 0.03 us -> 90.4 us
    all_gather x0 -> x3, blocking collectives: none -> 52 us  [the longest x1 20.7 us: on_device(): column = lax.all_gather(mine, 'expert', axis=0, tiled=True)]
    reduce_scatter x1, waiting for transfers between devices: 95.5 us -> 54.8 us  [on_device(): lax.psum_scatter(summed.astype(jnp.float32), 'expert', scatter_dimension=...]
    dot_general x3 -> x4, matrix products: 12 us -> 42.7 us  [the longest x1 15.4 us: on_device(): jnp.einsum('erf,efd->erd', hidden, down_weight, preferred_element_type=jn...]
    all_gather x1 -> x2, waiting for transfers between devices: 67.3 us -> 94.6 us  [the longest x1 51.8 us: on_device(): blended = lax.all_gather(own, 'dp', axis=1, tiled=True)]
    reshape x3 -> x0, local copies, waits for them, and re-layouts: 26.2 us -> none  [the longest x2 16.3 us: on_device(): outgoing.reshape(expert_groups, local_experts, capacity, model_width)]
  transfers between devices with their start and end apart: 3 -> 4, of which waited for: 3 -> 4; matrix products, arithmetic and copies ran while one was open for 0% -> 2% of each run, Pallas kernels for 0% -> 0%
where the time goes in v1:
time: 416 us; the launch traced here: 412 us
  waiting for transfers between devices  240 us (58%)
  blocking collectives  74.3 us (18%)
  matrix products  42.7 us (10%)
  local copies, waits for them, and re-layouts  29.2 us (7%)
  between operations  16.3 us (4%)
  other arithmetic  9.1 us (2%)
    unnamed x5, waiting for transfers between devices  90.4 us
    reduce_scatter x1, waiting for transfers between devices, on_device(): lax.psum_scatter(summed.astype(jnp.float32), 'expert', scatter_dimension=...  54.8 us
    all_gather x1, waiting for transfers between devices, on_device(): blended = lax.all_gather(own, 'dp', axis=1, tiled=True)  51.8 us
    all_gather x1, waiting for transfers between devices, on_device(): every = lax.all_gather(column, 'dp', axis=1, tiled=True)  42.8 us
    psum x1, blocking collectives, on_device(): loss_sum, token_total = lax.psum((local_loss, jnp.sum(weights)), 'expert')  22.3 us
    all_gather x1, blocking collectives, on_device(): column = lax.all_gather(mine, 'expert', axis=0, tiled=True)  20.7 us
    unnamed x11, local copies, waits for them, and re-layouts  16.8 us
    all_gather x1, blocking collectives, on_device(): ids = lax.all_gather(expert_ids, 'expert', axis=0, tiled=True)  16.7 us
  transfers between devices with their start and end apart: 4, of which 4 were waited for; matrix products, arithmetic and copies ran while one was open for 2% of the time, Pallas kernels for 0%

profile of v1, /device:TPU:32, one launch (start us, length us, event | category | flops | bytes accessed | tf_op | source)
XLA Modules:
  0.0 411.6 jit_solution(1104938401888615248)
XLA Ops:
  7.2 0.0 copy-start
  7.2 0.0 all-gather.3.cloned.1.call-start
  7.2 1.0 dynamic-slice_convert_fusion
  8.2 20.7 %all_gather.16 = bf16[2048,128]{1,0:T(8,128)(2,1)} all-gather(bf16[128,128]{1,0:T(8,128)(2,1)S(1)} %dynamic-slice_convert_fusion), channel_id=1, replica_groups=mesh['dp'=16,'expert'=16] {'expert'}, dimensions={0}, use_global_device_ids=true | all-gather | bytes 557056 | tf_op jit(solution)/shard_map/all_gather | solution.py:19
  28.9 0.0 all-gather.3.cloned.1.call-update
  28.9 0.0 reduce-scatter.7.cloned.1.call-start
  29.0 0.7 convert_element_type.41
  29.6 16.7 %all_gather.15 = s32[2048,8]{0,1:T(8,128)S(1)} all-gather(s32[128,8]{0,1:T(8,128)} %param.8), channel_id=1, replica_groups=mesh['dp'=16,'expert'=16] {'expert'}, dimensions={0}, use_global_device_ids=true | all-gather | bytes 69632 | tf_op jit(solution)/shard_map/all_gather | solution.py:21
  46.3 0.2 compare_reduce_fusion
  46.6 1.4 copy.28
  48.0 2.8 subtract_bitcast_fusion
  50.8 1.6 copy.30
  52.4 0.7 broadcast_multiply_fusion
  53.1 14.7 %all_gather.18 = f32[2048,8]{0,1:T(8,128)S(1)} all-gather(f32[128,8]{0,1:T(8,128)S(1)} %broadcast_multiply_fusion), channel_id=1, replica_groups=mesh['dp'=16,'expert'=16] {'expert'}, dimensions={0}, use_global_device_ids=true | all-gather | bytes 69632 | tf_op jit(solution)/shard_map/all_gather | solution.py:22
  67.7 0.2 fusion.16
  68.0 0.4 select_reduce_fusion
  68.4 42.8 %all-gather.3.cloned.1.call-done = bf16[2048,2048]{1,0:T(8,128)(2,1)} async-done(((bf16[2048,128]{1,0:T(8,128)(2,1)}), bf16[2048,2048]{1,0:T(8,128)(2,1)}) %all-gather.3.cloned.1.call-update) | async-done | bytes 8388624 | tf_op jit(solution)/shard_map/all_gather | solution.py:20
  111.2 8.9 %convert_bitcast_fusion = bf16[8,16,16,2048]{3,2,0,1:T(8,128)(2,1)} fusion(bf16[16,128,2048,1]{2,1,3,0:T(8,128)(2,1)} %bitcast.42, s32[16,8,128]{2,1,0:T(8,128)S(1)} %copy.30, pred[16,8,128]{2,1,0:T(8,128)(4,1)S(1)} %compare_bitcast_fusion), kind=kOutput, calls=%fused_computation.5 | convolution fusion | flops 1078460416 | bytes 16859136 | tf_op jit(solution)/shard_map/best,btf->ebsf/dot_general | solution.py:35
  120.1 0.0 copy-start.3
  120.1 8.4 %copy.31 = bf16[8,16,16,2048]{3,2,1,0:T(8,128)(2,1)} copy(bf16[8,16,16,2048]{3,2,0,1:T(8,128)(2,1)} %convert_bitcast_fusion) | data formatting | bytes 16777216 | tf_op jit(solution)/shard_map/convert_element_type | solution.py:37
  128.5 0.0 copy-done.3
  128.5 7.0 %fusion.23 = f32[8,256,96]{1,2,0:T(8,128)} fusion(bf16[8,256,2048]{2,1,0:T(8,128)(2,1)} %bitcast.37, bf16[8,96,2048]{2,1,0:T(8,128)(2,1)S(1)} %copy-done.3), kind=kOutput, calls=%fused_computation.35 | convolution fusion | flops 805306368 | bytes 12320768 | tf_op jit(solution)/shard_map/erd,efd->erf/dot_general | solution.py:39
  135.5 0.0 copy-done
  135.5 15.4 %fusion.7 = f32[8,256,2048]{2,1,0:T(8,128)} fusion(bf16[8,96,2048]{2,1,0:T(8,128)(2,1)S(1)} %copy-done, bf16[8,256,2048]{2,1,0:T(8,128)(2,1)} %bitcast.38, bf16[8,96,2048]{2,1,0:T(8,128)(2,1)} %param.12, f32[8,256,96]{1,2,0:T(8,128)} %fusion.23), kind=kOutput, calls=%fused_computation.8 | convolution fusion | flops 1611792384 | bytes 32243712 | tf_op jit(solution)/shard_map/erf,efd->erd/dot_general | solution.py:42
  150.9 11.4 %bitcast_convert_fusion = bf16[16,128,2048]{2,1,0:T(8,128)(2,1)} fusion(f32[8,16,16,2048]{3,2,1,0:T(8,128)} %bitcast.34, f32[8,16,16]{2,0,1:T(8,128)S(1)} %bitcast.40, s32[16,8,128]{2,1,0:T(8,128)S(1)} %copy.30, pred[16,8,128]{2,1,0:T(8,128)(4,1)S(1)} %compare_bitcast_fusion), kind=kOutput, calls=%fused_computation | convolution fusion | flops 1086849024 | bytes 25255936 | tf_op jit(solution)/shard_map/best,ebsf->btf/dot_general | solution.py:44
  162.3 0.0 copy-start.1
  162.3 12.5 %copy.35 = bf16[2048,2048]{0,1:T(8,128)(2,1)} copy(bf16[2048,2048]{1,0:T(8,128)(2,1)} %bitcast.36) | data formatting | bytes 16777216
  174.8 0.0 copy-start.2
  174.8 0.0 reduce-scatter.7.cloned.1.call-update
  174.8 0.0 reduce-scatter.5.cloned.1.call-start
  174.9 90.3 %reduce-scatter.7.cloned.1.call-done = bf16[128,2048]{1,0:T(8,128)(2,1)} async-done(((bf16[2048,2048]{1,0:T(8,128)(2,1)}), bf16[128,2048]{1,0:T(8,128)(2,1)}) %reduce-scatter.7.cloned.1.call-update) | async-done | bytes 524304
  265.2 2.0 copy.36
  267.2 2.1 convert_element_type.45
  269.3 0.0 reduce-scatter.5.cloned.1.call-update
  269.3 0.0 all-gather.5.cloned.1.call-start
  269.4 54.8 %reduce-scatter.5.cloned.1.call-done = f32[128,128]{1,0:T(8,128)} async-done(((f32[2048,128]{1,0:T(8,128)}), f32[128,128]{1,0:T(8,128)}) %reduce-scatter.5.cloned.1.call-update) | async-done | bytes 65552 | tf_op jit(solution)/shard_map/reduce_scatter | solution.py:48
  324.1 0.0 all-gather.5.cloned.1.call-update
  324.2 51.8 %all-gather.5.cloned.1.call-done = f32[128,2048]{1,0:T(8,128)} async-done(((f32[128,128]{1,0:T(8,128)}), f32[128,2048]{1,0:T(8,128)}) %all-gather.5.cloned.1.call-update) | async-done | bytes 1048592 | tf_op jit(solution)/shard_map/all_gather | solution.py:49
  376.0 1.4 multiply_reduce_fusion
  377.4 0.0 copy-done.2
  377.4 0.6 convert_reduce_fusion
  378.0 22.3 %all-reduce = (f32[]{:T(128)}, f32[]{:T(128)}) all-reduce(f32[]{:T(128)} %get-tuple-element.3, f32[]{:T(128)} %get-tuple-element.2), channel_id=1, replica_groups=mesh['dp'=16,'expert'=16] {'expert'}, use_global_device_ids=true, to_apply=%region_8.9 | all-reduce | flops 2 | bytes 16 | tf_op jit(solution)/shard_map/psum | solution.py:52
  401.6 2.3 copy.44
  403.9 0.0 copy-done.1
  (3 shorter events, 0.0 us)
Async XLA Ops:
  7.2 128.3 %copy-start = (bf16[8,96,2048]{2,1,0:T(8,128)(2,1)S(1)}, bf16[8,96,2048]{2,1,0:T(8,128)(2,1)}, u32[]{:S(2)}) copy-start(bf16[8,96,2048]{2,1,0:T(8,128)(2,1)} %param.13) | copy-start | bytes 9437188
  7.2 104.0 %all-gather.3.cloned.1.call-start = ((), (), s32[]{:S(2)}) async-start(), calls=%async_computation.2 | async-start | bytes 8912896 | tf_op jit(solution)/shard_map/all_gather | solution.py:20
  28.9 236.3 %reduce-scatter.7.cloned.1.call-start = ((), (), s32[]{:S(2)}) async-start(), calls=%async_computation.5 | async-start | bytes 8912896
  120.1 8.4 %copy-start.3 = (bf16[8,96,2048]{2,1,0:T(8,128)(2,1)S(1)}, bf16[8,96,2048]{2,1,0:T(8,128)(2,1)}, u32[]{:S(2)}) copy-start(bf16[8,96,2048]{2,1,0:T(8,128)(2,1)} %param.11) | copy-start | bytes 9437188
  162.3 241.6 %copy-start.1 = (bf16[8,96,2048]{2,1,0:T(8,128)(2,1)S(1)}, bf16[8,96,2048]{2,1,0:T(8,128)(2,1)}, u32[]{:S(2)}) copy-start(bf16[8,96,2048]{2,1,0:T(8,128)(2,1)} %param.13) | copy-start | bytes 9437188
  174.8 202.6 %copy-start.2 = (s32[128]{0:T(128)S(1)}, s32[128]{0:T(128)}, u32[]{:S(2)}) copy-start(s32[128]{0:T(128)} %param.10) | copy-start | bytes 1540
  174.8 149.3 %reduce-scatter.5.cloned.1.call-start = ((), (), s32[]{:S(2)}) async-start(), calls=%async_computation.3 | async-start | bytes 1114112 | tf_op jit(solution)/shard_map/reduce_scatter | solution.py:48
  269.3 106.6 %all-gather.5.cloned.1.call-start = ((), (), s32[]{:S(2)}) async-start(), calls=%async_computation.4 | async-start | bytes 1114112 | tf_op jit(solution)/shard_map/all_gather | solution.py:49
Sparse Core Ops, SparseCore 0:
  29.0 82.0 all-gather.2
  174.9 90.2 reduce-scatter.6
  269.4 54.6 reduce-scatter.4
  326.4 49.5 all-gather.4

commit v2 on v1

v2 whole, which is shorter than its diff:
```python
import jax
import jax.numpy as jnp
from jax import lax
from jax.experimental import pallas as pl
from jax.experimental.pallas import tpu as pltpu
from jax.sharding import PartitionSpec as P

MESH = pl.DeviceIdType.MESH
BF = jnp.bfloat16
F32 = jnp.float32
SLOTS = 16
ORDER = (0, 1, 7, 2, 6, 3, 5, 4)
POS = {dz: k for k, dz in enumerate(ORDER)}
GROUPS = ((0, 1, 7, 2), (6, 3, 5, 4))
XFIRST = {0: False, 1: True, 7: False, 2: True, 6: False, 3: True, 5: False, 4: True}
TURN = {0: 1, 1: 1, 7: -1, 2: -1, 6: 1, 3: 1, 5: -1, 4: -1}


def kernel(tok, meta, mask, gw, uw, dw, out, loss,
           TOK, META, X, W1, WD, SEL, STR, GS, PART, PX, PEX, RB, RA, ACCB, SUMB, ACCA, Q, ZR, FIN, LR, LS,
           wsem, zs, zr, ms, mr, as_, ar, bs, br, ps, pr, qs, qr, rbs, rbr, ras, rar, vs, vr, fs, fr, ls, lr):
    dp = lax.axis_index("dp")
    ex = lax.axis_index("expert")
    y, x = dp // 4, dp % 4
    z, c = ex // 2, ex % 2

    def peer(dz, rc):
        core = c if rc == 0 else 1 - c
        return {"dp": dp, "expert": ((z + dz) % 8) * 2 + core}

    def step(axis, d):
        if axis == "x":
            return {"dp": y * 4 + (x + d + 4) % 4, "expert": ex}
        return {"dp": ((y + d + 4) % 4) * 4 + x, "expert": ex}

    def remote(src, dst, ssem, rsem, dev):
        return pltpu.make_async_remote_copy(
            src_ref=src, dst_ref=dst, send_sem=ssem, recv_sem=rsem, device_id=dev, device_id_type=MESH)

    pending = []

    def send(src, dst, ssem, rsem, dev):
        cp = remote(src, dst, ssem, rsem, dev)
        cp.start()
        pending.append(cp)

    def arrive(dst, ssem, rsem):
        remote(dst, dst, ssem, rsem, peer(0, 1)).wait_recv()

    weights = [
        pltpu.make_async_copy(gw, W1.at[:, pl.ds(0, 96), :], wsem.at[0]),
        pltpu.make_async_copy(uw, W1.at[:, pl.ds(128, 96), :], wsem.at[1]),
        pltpu.make_async_copy(dw, WD.at[:, pl.ds(0, 96), :], wsem.at[2]),
    ]
    for w in weights:
        w.start()

    barrier = pltpu.get_barrier_semaphore()
    everyone = [peer(dz, rc) for dz in range(8) for rc in range(2) if (dz, rc) != (0, 0)]
    everyone += [step(axis, d) for axis in "xy" for d in (1, 2, 3)]
    for dev in everyone:
        pl.semaphore_signal(barrier, inc=1, device_id=dev, device_id_type=MESH)

    for i in range(4):
        for j in range(4):
            f = (i * 4 + j) * 128
            TOK[0, 0, i, j] = tok[:, f:f + 128].astype(BF)
    META[0] = meta[...]
    pl.semaphore_wait(barrier, len(everyone))

    for n, dz in enumerate(ORDER[1:]):
        back = (8 - dz) % 8
        send(TOK.at[0, 0, y, x], TOK.at[back, 0, y, x], zs.at[dz], zr.at[back], peer(dz, 0))
    for dz in ORDER:
        back = (8 - dz) % 8
        for rc in range(2):
            if (dz, rc) != (0, 0):
                k, kb = 2 * POS[dz] + rc, 2 * POS[back] + rc
                send(meta, META.at[kb], ms.at[k], mr.at[kb], peer(dz, rc))
    send(TOK.at[0, 0], TOK.at[0, 1], ps.at[0], pr.at[0], peer(0, 1))

    zero = jnp.zeros((32, 2048), BF)
    for e in range(8):
        W1[e, 96:128, :] = zero
        W1[e, 224:256, :] = zero
        WD[e, 96:128, :] = zero

    def near(dz):
        return ("x", "y", x, y) if XFIRST[dz] else ("y", "x", y, x)

    def piece(ref, dz, pos):
        pos = (pos + 4) % 4
        return ref.at[dz, 0, y, pos] if XFIRST[dz] else ref.at[dz, 0, pos, x]

    def bundle(ref, dz, pos):
        pos = (pos + 4) % 4
        return ref.at[dz, 0, pos] if XFIRST[dz] else ref.at[dz, 0, :, pos]

    def spread(part, dz, axis, me, ssem, rsem):
        send(part(TOK, dz, me), part(TOK, dz, me), ssem.at[dz, 0], rsem.at[dz, 0], step(axis, 1))
        send(part(TOK, dz, me), part(TOK, dz, me), ssem.at[dz, 1], rsem.at[dz, 1], step(axis, -1))

    def onward(part, dz, axis, me, ssem, rsem):
        s = TURN[dz]
        got = part(TOK, dz, me - s)
        arrive(got, ssem.at[dz, 2], rsem.at[dz, 0 if s == 1 else 1])
        send(got, got, ssem.at[dz, 2], rsem.at[dz, 2], step(axis, s))

    def complete(part, dz, me, ssem, rsem):
        s = TURN[dz]
        arrive(part(TOK, dz, me + s), ssem.at[dz, 2], rsem.at[dz, 1 if s == 1 else 0])
        arrive(part(TOK, dz, me + 2), ssem.at[dz, 2], rsem.at[dz, 2])

    rest = ORDER[1:]
    for dz in rest:
        a, b, ma, mb = near(dz)
        arrive(TOK.at[dz, 0, y, x], zs.at[0], zr.at[dz])
        spread(piece, dz, a, ma, as_, ar)
    for dz in rest:
        a, b, ma, mb = near(dz)
        onward(piece, dz, a, ma, as_, ar)
    for dz in rest:
        a, b, ma, mb = near(dz)
        complete(piece, dz, ma, as_, ar)
        spread(bundle, dz, b, mb, bs, br)

    for k in range(1, 16):
        arrive(META.at[k], ms.at[0], mr.at[k])
    row = lax.broadcasted_iota(jnp.int32, (128, 128), 0)
    col = lax.broadcasted_iota(jnp.int32, (128, 128), 1)
    before = (row < col).astype(F32).astype(BF)
    local = (lax.broadcasted_iota(jnp.int32, (8, 128), 0) + ex * 8).astype(F32)
    slot = lax.broadcasted_iota(jnp.int32, (8, SLOTS, 128), 1).astype(F32)

    def route(k, carry):
        m = META[k]
        named = jnp.zeros((8, 128), F32)
        gate = jnp.zeros((8, 128), F32)
        for i in range(8):
            hit = m[i:i + 1, :] == local
            named = jnp.where(hit, 1.0, named)
            gate = gate + jnp.where(hit, m[8 + i:9 + i, :], 0.0)
        rank = jnp.dot(named.astype(BF), before, preferred_element_type=F32)
        rank = jnp.where(named > 0.0, rank, -1.0)
        pick = jnp.broadcast_to(rank[:, None, :], (8, SLOTS, 128)) == slot
        one = jnp.where(pick, 1.0, 0.0).reshape(128, 128)
        SEL[k] = one.astype(BF)
        STR[k] = one.T.astype(BF)
        held = jnp.where(pick, jnp.broadcast_to(gate[:, None, :], (8, SLOTS, 128)), 0.0)
        GS[:, pl.ds(pl.multiple_of(k * SLOTS, SLOTS), SLOTS), :] = jnp.broadcast_to(
            jnp.sum(held, axis=2, keepdims=True), (8, SLOTS, 128))
        return carry

    lax.fori_loop(0, 16, route, 0)

    for dz in rest:
        a, b, ma, mb = near(dz)
        onward(bundle, dz, b, mb, bs, br)
    for dz in rest:
        a, b, ma, mb = near(dz)
        complete(bundle, dz, mb, bs, br)
        send(TOK.at[dz, 0], TOK.at[dz, 1], ps.at[dz], pr.at[dz], peer(0, 1))

    for w in weights:
        w.wait()

    def select(dz, rc):
        k = 2 * POS[dz] + rc
        pick = SEL[k]
        for i in range(4):
            rhs = jnp.concatenate([TOK[dz, rc, i, j] for j in range(4)], axis=1)
            got = jnp.dot(pick, rhs, preferred_element_type=F32).astype(BF)
            X[:, k * SLOTS:(k + 1) * SLOTS, i * 512:(i + 1) * 512] = got.reshape(8, SLOTS, 512)

    def ffn(group):
        lo = 2 * SLOTS * POS[group[0]]
        hi = lo + 2 * SLOTS * len(group)

        def one(e, carry):
            pre = lax.dot_general(X[e, lo:hi, :], W1[e], (((1,), (1,)), ((), ())), preferred_element_type=F32)
            g, u = pre[:, :128], pre[:, 128:]
            h = (g / (1.0 + jnp.exp(-g)) * u).astype(BF)
            scale = GS[e, lo:hi, :]
            scale = jnp.concatenate([scale] * 4, axis=1)
            for i in range(4):
                o = jnp.dot(h, WD[e, :, i * 512:(i + 1) * 512], preferred_element_type=F32)
                X[e, lo:hi, i * 512:(i + 1) * 512] = (o * scale).astype(BF)
            return carry

        lax.fori_loop(0, 8, one, 0)

    def combine(dz, rc, i):
        k = 2 * POS[dz] + rc
        rhs = X[:, k * SLOTS:(k + 1) * SLOTS, i * 512:(i + 1) * 512].reshape(128, 512)
        return jnp.dot(STR[k], rhs, preferred_element_type=F32)

    def home(ref, dz, pos):
        pos = (pos + 4) % 4
        return ref.at[dz, pos] if XFIRST[dz] else ref.at[dz, :, pos]

    for group in GROUPS:
        for dz in group:
            select(dz, 0)
        for dz in group:
            arrive(TOK.at[dz, 1], ps.at[0], pr.at[dz])
            select(dz, 1)
        ffn(group)
        for dz in group:
            for i in range(4):
                got = combine(dz, 1, i).astype(BF)
                for j in range(4):
                    PX[dz, i, j] = got[:, j * 128:(j + 1) * 128]
            send(PX.at[dz], PEX.at[dz], qs.at[dz], qr.at[dz], peer(0, 1))
        for dz in group:
            a, b, ma, mb = near(dz)
            s = TURN[dz]
            arrive(PEX.at[dz], qs.at[dz], qr.at[dz])
            for i in range(4):
                got = combine(dz, 0, i)
                for j in range(4):
                    PART[dz, i, j] = (got[:, j * 128:(j + 1) * 128] + PEX[dz, i, j].astype(F32)).astype(BF)
            send(home(PART, dz, mb + 2), RB.at[dz, 0], rbs.at[dz, 0], rbr.at[dz, 0], step(b, s))
            send(home(PART, dz, mb - s), RB.at[dz, 1], rbs.at[dz, 1], rbr.at[dz, 1], step(b, -s))

    for dz in ORDER:
        a, b, ma, mb = near(dz)
        s = TURN[dz]
        arrive(RB.at[dz, 0], rbs.at[dz, 0], rbr.at[dz, 0])
        ACCB[dz] = (RB[dz, 0].astype(F32) + home(PART, dz, mb + s)[...].astype(F32)).astype(BF)
        send(ACCB.at[dz], RB.at[dz, 2], rbs.at[dz, 2], rbr.at[dz, 2], step(b, s))
    for dz in ORDER:
        a, b, ma, mb = near(dz)
        s = TURN[dz]
        arrive(RB.at[dz, 1], rbs.at[dz, 1], rbr.at[dz, 1])
        arrive(RB.at[dz, 2], rbs.at[dz, 2], rbr.at[dz, 2])
        SUMB[dz] = (home(PART, dz, mb)[...].astype(F32) + RB[dz, 1].astype(F32) + RB[dz, 2].astype(F32)).astype(BF)
        send(SUMB.at[dz, (ma + 2) % 4], RA.at[dz, 0], ras.at[dz, 0], rar.at[dz, 0], step(a, s))
        send(SUMB.at[dz, (ma - s + 4) % 4], RA.at[dz, 1], ras.at[dz, 1], rar.at[dz, 1], step(a, -s))
    for dz in ORDER:
        a, b, ma, mb = near(dz)
        s = TURN[dz]
        arrive(RA.at[dz, 0], ras.at[dz, 0], rar.at[dz, 0])
        ACCA[dz] = (RA[dz, 0].astype(F32) + SUMB[dz, (ma + s + 4) % 4].astype(F32)).astype(BF)
        send(ACCA.at[dz], RA.at[dz, 2], ras.at[dz, 2], rar.at[dz, 2], step(a, s))
    for dz in ORDER[1:] + ORDER[:1]:
        a, b, ma, mb = near(dz)
        arrive(RA.at[dz, 1], ras.at[dz, 1], rar.at[dz, 1])
        arrive(RA.at[dz, 2], ras.at[dz, 2], rar.at[dz, 2])
        total = SUMB[dz, ma].astype(F32) + RA[dz, 1].astype(F32) + RA[dz, 2].astype(F32)
        if dz:
            Q[dz] = total.astype(BF)
            back = (8 - dz) % 8
            send(Q.at[dz], ZR.at[back], vs.at[dz], vr.at[back], peer(dz, 0))
    for dz in ORDER[1:]:
        arrive(ZR.at[dz], vs.at[0], vr.at[dz])
        total = total + ZR[dz].astype(F32)
    FIN[y, x] = total.astype(BF)

    for d in (1, 3, 2):
        send(FIN.at[y, x], FIN.at[y, x], fs.at[d], fr.at[d], step("x", d))
    for d in (1, 3, 2):
        arrive(FIN.at[y, (x - d + 4) % 4], fs.at[0], fr.at[d])
    for d in (1, 3, 2):
        send(FIN.at[y], FIN.at[y], fs.at[4 + d], fr.at[4 + d], step("y", d))
    for d in (1, 3, 2):
        arrive(FIN.at[(y - d + 4) % 4], fs.at[0], fr.at[4 + d])

    squares = jnp.zeros((8, 128), F32)
    for i in range(4):
        for j in range(4):
            v = FIN[i, j]
            f = (i * 4 + j) * 128
            out[:, f:f + 128] = v
            w = v.astype(F32)
            squares = squares + jnp.sum((w * w).reshape(16, 8, 128), axis=0)
    LS[0:8] = squares
    LS[8:16] = mask[...]
    for dz in ORDER:
        back = (8 - dz) % 8
        for rc in range(2):
            if (dz, rc) != (0, 0):
                k, kb = 2 * POS[dz] + rc, 2 * POS[back] + rc
                send(LS, LR.at[kb], ls.at[k], lr.at[kb], peer(dz, rc))
    LR[0] = LS[...]
    for k in range(1, 16):
        arrive(LR.at[k], ls.at[0], lr.at[k])
    gathered = jnp.sum(LR[...], axis=0)
    top = jnp.sum(jnp.sum(gathered[0:8], axis=0, keepdims=True), axis=1, keepdims=True) * (1.0 / 2048.0)
    count = jnp.sum(jnp.sum(gathered[8:16], axis=0, keepdims=True), axis=1, keepdims=True)
    loss[...] = jnp.broadcast_to(top / count, (8, 128))

    for cp in pending:
        cp.wait_send()


def on_device(tokens, expert_ids, gate_values, valid_mask, gate_weight, up_weight, down_weight):
    weights = valid_mask.astype(F32)
    meta = jnp.concatenate([expert_ids.astype(F32).T, (gate_values * weights[:, None]).T], axis=0)
    mask = jnp.concatenate([weights[None, :], jnp.zeros((7, 128), F32)], axis=0)
    vmem = pl.BlockSpec(memory_space=pltpu.VMEM)
    hbm = pl.BlockSpec(memory_space=pl.ANY)
    dma = pltpu.SemaphoreType.DMA
    out, loss = pl.pallas_call(
        kernel,
        out_shape=(jax.ShapeDtypeStruct((128, 2048), BF), jax.ShapeDtypeStruct((8, 128), F32)),
        in_specs=[vmem, vmem, vmem, hbm, hbm, hbm],
        out_specs=(vmem, vmem),
        scratch_shapes=[
            pltpu.VMEM((8, 2, 4, 4, 128, 128), BF),
            pltpu.VMEM((16, 16, 128), F32),
            pltpu.VMEM((8, 256, 2048), BF),
            pltpu.VMEM((8, 256, 2048), BF),
            pltpu.VMEM((8, 128, 2048), BF),
            pltpu.VMEM((16, 128, 128), BF),
            pltpu.VMEM((16, 128, 128), BF),
            pltpu.VMEM((8, 256, 128), F32),
            pltpu.VMEM((8, 4, 4, 128, 128), BF),
            pltpu.VMEM((8, 4, 4, 128, 128), BF),
            pltpu.VMEM((8, 4, 4, 128, 128), BF),
            pltpu.VMEM((8, 3, 4, 128, 128), BF),
            pltpu.VMEM((8, 3, 128, 128), BF),
            pltpu.VMEM((8, 4, 128, 128), BF),
            pltpu.VMEM((8, 4, 128, 128), BF),
            pltpu.VMEM((8, 128, 128), BF),
            pltpu.VMEM((8, 128, 128), BF),
            pltpu.VMEM((8, 128, 128), BF),
            pltpu.VMEM((4, 4, 128, 128), BF),
            pltpu.VMEM((16, 16, 128), F32),
            pltpu.VMEM((16, 128), F32),
            dma((3,)), dma((8,)), dma((8,)), dma((16,)), dma((16,)),
            dma((8, 3)), dma((8, 3)), dma((8, 3)), dma((8, 3)),
            dma((8,)), dma((8,)), dma((8,)), dma((8,)),
            dma((8, 3)), dma((8, 3)), dma((8, 3)), dma((8, 3)),
            dma((8,)), dma((8,)), dma((8,)), dma((8,)), dma((16,)), dma((16,)),
        ],
        compiler_params=pltpu.CompilerParams(
            collective_id=0, has_side_effects=True, vmem_limit_bytes=62 * 1024 * 1024),
    )(tokens, meta, mask, gate_weight, up_weight, down_weight)
    return out.astype(F32), loss[0, 0]


def solution(mesh):
    return jax.shard_map(
        on_device,
        mesh=mesh,
        in_specs=(
            P("expert", None),
            P("expert", None),
            P("expert", None),
            P("expert"),
            P("expert", "dp", None),
            P("expert", "dp", None),
            P("expert", "dp", None),
        ),
        out_specs=(P("expert", None), P()),
        check_vma=False,
    )
```

time: 416 us -> 123 us (0.30)
  waiting for transfers between devices: 240 us -> 0 us
  Pallas kernels: 0 us -> 114 us
  blocking collectives: 74.3 us -> 0 us
  matrix products: 42.7 us -> 0 us
  local copies, waits for them, and re-layouts: 29.2 us -> 1.78 us
  between operations: 16.3 us -> 0.64 us
  other arithmetic: 9.1 us -> 4.76 us
    pallas_call x0 -> x1, Pallas kernels: none -> 114 us  [on_device(): pl.pallas_call(kernel, out_shape=(jax.ShapeDtypeStruct((128, 2048), BF),...]
    all_gather x2 -> x0, waiting for transfers between devices: 94.6 us -> none  [the longest x1 51.8 us: on_device(): blended = lax.all_gather(own, 'dp', axis=1, tiled=True)]
    unnamed x5 -> x0, waiting for transfers between devices: 90.4 us -> none
    reduce_scatter x1 -> x0, waiting for transfers between devices: 54.8 us -> none  [on_device(): lax.psum_scatter(summed.astype(jnp.float32), 'expert', scatter_dimension=...]
    all_gather x3 -> x0, blocking collectives: 52 us -> none  [the longest x1 20.7 us: on_device(): column = lax.all_gather(mine, 'expert', axis=0, tiled=True)]
    dot_general x4 -> x0, matrix products: 42.7 us -> none  [the longest x1 15.4 us: on_device(): jnp.einsum('erf,efd->erd', hidden, down_weight, preferred_element_type=jn...]
    psum x1 -> x0, blocking collectives: 22.3 us -> none  [on_device(): loss_sum, token_total = lax.psum((local_loss, jnp.sum(weights)), 'expert')]
    unnamed x11 -> x0, local copies, waits for them, and re-layouts: 16.8 us -> none
  transfers between devices with their start and end apart: 4 -> 0, of which waited for: 4 -> 0; matrix products, arithmetic and copies ran while one was open for 2% -> 0% of each run, Pallas kernels for 0% -> 0%
where the time goes in v2:
time: 123 us; the launch traced here: 122 us
  Pallas kernels  114 us (93%)
  other arithmetic  4.76 us (4%)
  local copies, waits for them, and re-layouts  1.78 us (1%)
    pallas_call x1, Pallas kernels, on_device(): pl.pallas_call(kernel, out_shape=(jax.ShapeDtypeStruct((128, 2048), BF),...  114 us

profile of v2, /device:TPU:32, one launch (start us, length us, event | category | flops | bytes accessed | tf_op | source)
XLA Modules:
  0.0 121.6 jit_solution(10758592474206040282)
XLA Ops:
  0.6 0.7 convert_bitcast_fusion.1
  1.3 0.6 concatenate.7.mask
  1.9 0.7 multiply_bitcast_fusion
  2.6 0.7 convert_bitcast_fusion
  3.3 0.6 pad_maximum_fusion.meta
  3.9 114.4 %shard_map.86 = (bf16[128,2048]{1,0:T(8,128)(2,1)}, f32[8,128]{1,0:T(8,128)}) custom-call(f32[128,2048]{1,0:T(8,128)} %tok.1, f32[16,128]{1,0:T(8,128)} %pad_maximum_fusion.meta, f32[8,128]{1,0:T(8,128)} %concatenate.7.mask, bf16[8,96,2048]{2,1,0:T(8,128)(2,1)} %gw.1, bf16[8,96,2048]{2,1,0:T(8,128)(2,1)} %uw.1, bf16[8,96,2048]{2,1,0:T(8,128)(2,1)} %dw.1), custom_call_target="tpu_custom_call" | custom-call | tf_op jit(solution)/shard_map/pallas_call | solution.py:303
  118.3 1.2 slice.3
  119.5 2.1 %convert_element_type.11 = f32[128,2048]{1,0:T(8,128)} convert(bf16[128,2048]{1,0:T(8,128)(2,1)} %get-tuple-element.4) | non-fusion elementwise | flops 262144 | bytes 1572864 | tf_op jit(solution)/shard_map/convert_element_type | solution.py:339

commit v3 on v1

v3 whole, which is shorter than its diff:
```python
import jax
import jax.numpy as jnp
from jax import lax
from jax.experimental import pallas as pl
from jax.experimental.pallas import tpu as pltpu
from jax.sharding import PartitionSpec as P

MESH = pl.DeviceIdType.MESH
BF = jnp.bfloat16
F32 = jnp.float32
SLOTS = 16
ORDER = (0, 2, 6, 3, 5, 4, 1, 7)
POS = {dz: k for k, dz in enumerate(ORDER)}
GZ, G0, G1 = (0,), (2, 6, 3, 5), (4, 1, 7)
PLANE = (2, 6, 3, 5, 4)
XFIRST = {0: False, 2: True, 6: False, 3: True, 5: False, 4: True, 1: False, 7: True}


def kernel(ids, gates, mask, tok, gw, uw, dw, out, loss,
           TOKF, TOK, MINE, META, X, H, W1, WD, SEL, STR, GS, PART, PX, PEX, RB, RA, ACCB, SUMB, Q, ZR, FIN, LS, LR, LT, LX, LY,
           wsem, zs, zr, ms, mr, as_, ar, bs, br, ps, pr, qs, qr, rbs, rbr, ras, rar, vs, vr, fs, fr, ls, lr):
    dp = lax.axis_index("dp")
    ex = lax.axis_index("expert")
    y, x = dp // 4, dp % 4
    z, c = ex // 2, ex % 2

    def peer(dz, rc):
        core = c if rc == 0 else 1 - c
        return {"dp": dp, "expert": ((z + dz) % 8) * 2 + core}

    def step(axis, d):
        if axis == "x":
            return {"dp": y * 4 + (x + d + 4) % 4, "expert": ex}
        return {"dp": ((y + d + 4) % 4) * 4 + x, "expert": ex}

    def remote(src, dst, ssem, rsem, dev):
        return pltpu.make_async_remote_copy(
            src_ref=src, dst_ref=dst, send_sem=ssem, recv_sem=rsem, device_id=dev, device_id_type=MESH)

    pending = []

    def send(src, dst, ssem, rsem, dev):
        cp = remote(src, dst, ssem, rsem, dev)
        cp.start()
        pending.append(cp)

    def arrive(dst, ssem, rsem):
        remote(dst, dst, ssem, rsem, peer(0, 1)).wait_recv()

    load = pltpu.make_async_copy(tok, TOKF, wsem.at[3])
    load.start()

    barrier = pltpu.get_barrier_semaphore()
    everyone = [peer(dz, rc) for dz in range(8) for rc in range(2) if (dz, rc) != (0, 0)]
    everyone += [step(axis, d) for axis in "xy" for d in (1, 2, 3)]
    for dev in everyone:
        pl.semaphore_signal(barrier, inc=1, device_id=dev, device_id_type=MESH)

    weights = [
        pltpu.make_async_copy(gw, W1.at[:, pl.ds(0, 96), :], wsem.at[0]),
        pltpu.make_async_copy(uw, W1.at[:, pl.ds(128, 96), :], wsem.at[1]),
        pltpu.make_async_copy(dw, WD.at[:, pl.ds(0, 96), :], wsem.at[2]),
    ]

    valid = jnp.broadcast_to(mask[...], (8, 128)) > 0
    MINE[0:8] = jnp.where(valid, ids[...], -1).astype(F32)
    MINE[8:16] = gates[...]
    META[0] = MINE[...]

    load.wait()
    for w in weights:
        w.start()
    for i in range(4):
        for j in range(4):
            f = (i * 4 + j) * 128
            TOK[0, 0, i, j] = TOKF[:, f:f + 128].astype(BF)
    pl.semaphore_wait(barrier, len(everyone))

    def back(dz):
        return (8 - dz) % 8

    def meta(dz):
        send(MINE, META.at[2 * POS[back(dz)]], ms.at[dz], mr.at[2 * POS[back(dz)]], peer(dz, 0))

    def slice_to(dz):
        send(TOK.at[0, 0, y, x], TOK.at[back(dz), 0, y, x], zs.at[dz], zr.at[back(dz)], peer(dz, 0))

    send(MINE, META.at[1], ms.at[0], mr.at[1], peer(0, 1))
    slice_to(2)
    slice_to(6)
    send(TOK.at[0, 0], TOK.at[0, 1], ps.at[0], pr.at[0], peer(0, 1))
    for dz in PLANE[2:]:
        slice_to(dz)
    for dz in ORDER[1:]:
        meta(dz)

    def whole():
        send(TOK.at[0, 0], TOK.at[7, 0], zs.at[1], zr.at[7], peer(1, 0))
        send(TOK.at[0, 0], TOK.at[1, 0], zs.at[7], zr.at[1], peer(7, 0))

    zero = jnp.zeros((32, 2048), BF)
    for e in range(8):
        W1[e, 96:128, :] = zero
        W1[e, 224:256, :] = zero
        WD[e, 96:128, :] = zero

    def near(dz):
        return ("x", "y", x, y) if XFIRST[dz] else ("y", "x", y, x)

    def wrap(pos):
        return (pos + 8) % 4

    def piece(dz, pos):
        return TOK.at[dz, 0, y, wrap(pos)] if XFIRST[dz] else TOK.at[dz, 0, wrap(pos), x]

    def bundle_half(dz, pos, h):
        two = pl.ds(2 * h, 2)
        return TOK.at[dz, 0, wrap(pos), two] if XFIRST[dz] else TOK.at[dz, 0, two, wrap(pos)]

    def t1(dz):
        a, b, ma, mb = near(dz)
        arrive(TOK.at[dz, 0, y, x], zs.at[dz], zr.at[dz])
        for d in (2, 1, 3):
            send(piece(dz, ma), piece(dz, ma), as_.at[dz, d - 1], ar.at[dz, d - 1], step(a, d))

    def t3(dz):
        a, b, ma, mb = near(dz)
        for d in (1, 3, 2):
            arrive(piece(dz, ma - d), as_.at[dz, d - 1], ar.at[dz, d - 1])
        for n, h, d in ((0, 0, 1), (1, 1, -1), (2, 1, 1), (3, 0, -1)):
            send(bundle_half(dz, mb, h), bundle_half(dz, mb, h), bs.at[dz, n], br.at[dz, n], step(b, d))

    def t4(dz):
        a, b, ma, mb = near(dz)
        for n, h, d in ((0, 0, 1), (1, 1, -1)):
            got = bundle_half(dz, mb - d, h)
            arrive(got, bs.at[dz, n], br.at[dz, n])
            send(got, got, bs.at[dz, 4 + n], br.at[dz, 4 + n], step(b, d))

    def t5(dz):
        a, b, ma, mb = near(dz)
        if dz in PLANE:
            for n, h, d in ((2, 1, 1), (3, 0, -1), (4, 0, 2), (5, 1, -2)):
                arrive(bundle_half(dz, mb - d, h), bs.at[dz, n], br.at[dz, n])
        else:
            arrive(TOK.at[dz, 0], zs.at[dz], zr.at[dz])
        send(TOK.at[dz, 0], TOK.at[dz, 1], ps.at[dz], pr.at[dz], peer(0, 1))

    row = lax.broadcasted_iota(jnp.int32, (128, 128), 0)
    col = lax.broadcasted_iota(jnp.int32, (128, 128), 1)
    before = (row < col).astype(F32).astype(BF)
    local = (lax.broadcasted_iota(jnp.int32, (8, 128), 0) + ex * 8).astype(F32)
    slot = lax.broadcasted_iota(jnp.int32, (8, SLOTS, 128), 1).astype(F32)

    def route(k, carry):
        m = META[k]
        named = jnp.zeros((8, 128), F32)
        gate = jnp.zeros((8, 128), F32)
        for i in range(8):
            hit = m[i:i + 1, :] == local
            named = jnp.where(hit, 1.0, named)
            gate = gate + jnp.where(hit, m[8 + i:9 + i, :], 0.0)
        rank = jnp.dot(named.astype(BF), before, preferred_element_type=F32)
        rank = jnp.where(named > 0.0, rank, -1.0)
        pick = jnp.broadcast_to(rank[:, None, :], (8, SLOTS, 128)) == slot
        one = jnp.where(pick, 1.0, 0.0).reshape(128, 128)
        SEL[k] = one.astype(BF)
        STR[k] = one.T.astype(BF)
        held = jnp.where(pick, jnp.broadcast_to(gate[:, None, :], (8, SLOTS, 128)), 0.0)
        GS[:, pl.ds(pl.multiple_of(k * SLOTS, SLOTS), SLOTS), :] = jnp.broadcast_to(
            jnp.sum(held, axis=2, keepdims=True), (8, SLOTS, 128))
        return carry

    def metas():
        for dz in ORDER[1:]:
            arrive(META.at[2 * POS[dz]], ms.at[dz], mr.at[2 * POS[dz]])
        for dz in ORDER[1:]:
            k = 2 * POS[dz]
            send(META.at[k], META.at[k + 1], ms.at[8 + dz], mr.at[k + 1], peer(0, 1))
        for dz in ORDER[1:]:
            k = 2 * POS[dz]
            arrive(META.at[k + 1], ms.at[8 + dz], mr.at[k + 1])
        lax.fori_loop(2, 16, route, 0)

    def own_plane():
        arrive(META.at[1], ms.at[0], mr.at[1])
        lax.fori_loop(0, 2, route, 0)

    def select(dz, rc):
        if rc:
            arrive(TOK.at[dz, 1], ps.at[dz], pr.at[dz])
        k = 2 * POS[dz] + rc
        pick = SEL[k]
        for i in range(4):
            rhs = jnp.concatenate([TOK[dz, rc, i, j] for j in range(4)], axis=1)
            got = jnp.dot(pick, rhs, preferred_element_type=F32).astype(BF)
            X[:, k * SLOTS:(k + 1) * SLOTS, i * 512:(i + 1) * 512] = got.reshape(8, SLOTS, 512)

    def span(group):
        lo = 2 * SLOTS * POS[group[0]]
        return lo, lo + 2 * SLOTS * len(group)

    def ups(group, first, last):
        lo, hi = span(group)

        def one(e, carry):
            pre = lax.dot_general(X[e, lo:hi, :], W1[e], (((1,), (1,)), ((), ())), preferred_element_type=F32)
            g, u = pre[:, :128], pre[:, 128:]
            H[e, lo:hi, :] = (g / (1.0 + jnp.exp(-g)) * u).astype(BF)
            return carry

        lax.fori_loop(first, last, one, 0, unroll=2)

    def downs(group, first, last):
        lo, hi = span(group)

        def one(e, carry):
            h = H[e, lo:hi, :]
            scale = GS[e, lo:hi, :]
            scale = jnp.concatenate([scale] * 4, axis=1)
            for i in range(4):
                o = jnp.dot(h, WD[e, :, i * 512:(i + 1) * 512], preferred_element_type=F32)
                X[e, lo:hi, i * 512:(i + 1) * 512] = (o * scale).astype(BF)
            return carry

        lax.fori_loop(first, last, one, 0, unroll=2)

    def combine(dz, rc, i):
        k = 2 * POS[dz] + rc
        rhs = X[:, k * SLOTS:(k + 1) * SLOTS, i * 512:(i + 1) * 512].reshape(128, 512)
        return jnp.dot(STR[k], rhs, preferred_element_type=F32)

    def give(dz):
        for i in range(4):
            got = combine(dz, 1, i).astype(BF)
            for j in range(4):
                PX[dz, i, j] = got[:, j * 128:(j + 1) * 128]
        send(PX.at[dz], PEX.at[dz], qs.at[dz], qr.at[dz], peer(0, 1))

    def home(dz, pos, h):
        two = pl.ds(2 * h, 2)
        return PART.at[dz, wrap(pos), two] if XFIRST[dz] else PART.at[dz, two, wrap(pos)]

    def plus(*refs):
        total = refs[0][...].astype(F32)
        for ref in refs[1:]:
            total = total + ref[...].astype(F32)
        return total

    def r1(dz):
        a, b, ma, mb = near(dz)
        arrive(PEX.at[dz], qs.at[dz], qr.at[dz])
        for i in range(4):
            got = combine(dz, 0, i)
            for j in range(4):
                PART[dz, i, j] = (got[:, j * 128:(j + 1) * 128] + PEX[dz, i, j].astype(F32)).astype(BF)
        send(home(dz, mb + 2, 0), RB.at[dz, 0], rbs.at[dz, 0], rbr.at[dz, 0], step(b, 1))
        send(home(dz, mb + 2, 1), RB.at[dz, 1], rbs.at[dz, 1], rbr.at[dz, 1], step(b, -1))
        send(home(dz, mb - 1, 0), RB.at[dz, 3], rbs.at[dz, 3], rbr.at[dz, 3], step(b, -1))
        send(home(dz, mb + 1, 1), RB.at[dz, 4], rbs.at[dz, 4], rbr.at[dz, 4], step(b, 1))

    def r2(dz):
        a, b, ma, mb = near(dz)
        for n, d in ((0, 1), (1, -1)):
            arrive(RB.at[dz, n], rbs.at[dz, n], rbr.at[dz, n])
            ACCB[dz, n] = plus(RB.at[dz, n], home(dz, mb + d, n)).astype(BF)
        for n, d, m in ((0, 1, 2), (1, -1, 5)):
            send(ACCB.at[dz, n], RB.at[dz, m], rbs.at[dz, m], rbr.at[dz, m], step(b, d))

    def r3(dz):
        a, b, ma, mb = near(dz)
        for n in (3, 4, 2, 5):
            arrive(RB.at[dz, n], rbs.at[dz, n], rbr.at[dz, n])
        SUMB[dz, 0:2] = plus(home(dz, mb, 0), RB.at[dz, 2], RB.at[dz, 3]).astype(BF)
        SUMB[dz, 2:4] = plus(home(dz, mb, 1), RB.at[dz, 4], RB.at[dz, 5]).astype(BF)
        for d in (2, 1, 3):
            send(SUMB.at[dz, wrap(ma + d)], RA.at[dz, d - 1], ras.at[dz, d - 1], rar.at[dz, d - 1], step(a, d))

    def r5(dz):
        a, b, ma, mb = near(dz)
        for d in (1, 3, 2):
            arrive(RA.at[dz, d - 1], ras.at[dz, d - 1], rar.at[dz, d - 1])
        Q[dz] = plus(SUMB.at[dz, ma], RA.at[dz, 0], RA.at[dz, 1], RA.at[dz, 2])
        if dz:
            ZR[8 + dz] = Q[dz].astype(BF)
            send(ZR.at[8 + dz], ZR.at[back(dz)], vs.at[dz], vr.at[back(dz)], peer(dz, 0))

    def each(task, group):
        for dz in group:
            task(dz)


    own_plane()
    select(0, 0)
    each(t1, (2, 6))
    select(0, 1)
    for w in weights:
        w.wait()
    ups(GZ, 0, 4)
    each(t1, (3, 5))
    each(t3, (2, 6))
    ups(GZ, 4, 8)
    t1(4)
    whole()
    each(t4, (2, 6))
    each(t3, (3, 5))
    downs(GZ, 0, 8)
    give(0)
    metas()
    each(t5, (2, 6))
    each(t4, (3, 5))
    t3(4)
    r1(0)
    select(2, 0)
    select(6, 0)
    each(t5, (3, 5))
    select(2, 1)
    select(6, 1)
    t4(4)
    r2(0)
    select(3, 0)
    select(5, 0)
    select(3, 1)
    select(5, 1)
    ups(G0, 0, 4)
    t5(4)
    r3(0)
    ups(G0, 4, 8)
    downs(G0, 0, 8)
    each(give, G0)
    each(t5, (1, 7))
    select(4, 0)
    select(4, 1)
    select(1, 0)
    select(7, 0)
    each(r1, G0)
    select(1, 1)
    select(7, 1)
    r5(0)
    ups(G1, 0, 4)
    each(r2, G0)
    ups(G1, 4, 8)
    downs(G1, 0, 4)
    each(r3, G0)
    downs(G1, 4, 8)
    each(give, G1)
    each(r5, G0)
    each(r1, G1)
    each(r2, G1)
    each(r3, G1)
    each(r5, G1)
    total = Q[0]
    for dz in ORDER[1:]:
        arrive(ZR.at[dz], vs.at[dz], vr.at[dz])
        total = total + ZR[dz].astype(F32)
    FIN[0, y, x] = total[0:64].astype(BF)
    FIN[1, y, x] = total[64:128].astype(BF)

    def strip(h, first, pos):
        if first:
            return FIN.at[0, y, wrap(pos)] if h == 0 else FIN.at[1, wrap(pos), x]
        return FIN.at[0, wrap(pos)] if h == 0 else FIN.at[1, :, wrap(pos)]

    for first in (True, False):
        base = 0 if first else 8
        legs = (("x", x), ("y", y)) if first else (("y", y), ("x", x))
        for d in (1, 3, 2):
            for h, (axis, me) in enumerate(legs):
                n = base + 4 * h + d
                send(strip(h, first, me), strip(h, first, me), fs.at[n], fr.at[n], step(axis, d))
        if first:
            LS[...] = jnp.sum((total * total).reshape(16, 8, 128), axis=0)
            for dz in ORDER:
                for rc in range(2):
                    if (dz, rc) != (0, 0):
                        k, kb = 2 * POS[dz] + rc, 2 * POS[back(dz)] + rc
                        send(LS, LR.at[kb], ls.at[k], lr.at[kb], peer(dz, rc))
            LR[0] = LS[...]
        for d in (1, 3, 2):
            for h, (axis, me) in enumerate(legs):
                n = base + 4 * h + d
                arrive(strip(h, first, me - d), fs.at[n], fr.at[n])
        if first:
            continue

    for k in range(1, 16):
        arrive(LR.at[k], ls.at[k], lr.at[k])
    LT[0] = jnp.sum(LR[...], axis=0)
    for d in (1, 3, 2):
        send(LT.at[0], LX.at[d], ls.at[16 + d], lr.at[16 + d], step("x", d))
    for i in range(4):
        for j in range(4):
            f = (i * 4 + j) * 128
            out[0:64, f:f + 128] = FIN[0, i, j].astype(out.dtype)
            out[64:128, f:f + 128] = FIN[1, i, j].astype(out.dtype)
    LX[0] = LT[0]
    for d in (1, 3, 2):
        arrive(LX.at[d], ls.at[16 + d], lr.at[16 + d])
    LT[1] = jnp.sum(LX[...], axis=0)
    for d in (1, 3, 2):
        send(LT.at[1], LY.at[d], ls.at[20 + d], lr.at[20 + d], step("y", d))
    count = jnp.sum(jnp.where(META[...][:, 0:1, :] >= 0.0, 1.0, 0.0), axis=0)
    count = jnp.sum(count, axis=1, keepdims=True)
    LY[0] = LT[1]
    for d in (1, 3, 2):
        arrive(LY.at[d], ls.at[20 + d], lr.at[20 + d])
    top = jnp.sum(LY[...], axis=0)
    top = jnp.sum(jnp.sum(top, axis=0, keepdims=True), axis=1, keepdims=True) * (1.0 / 2048.0)
    loss[...] = top / count

    for cp in pending:
        cp.wait_send()


def on_device(tokens, expert_ids, gate_values, valid_mask, gate_weight, up_weight, down_weight):
    vmem = pl.BlockSpec(memory_space=pltpu.VMEM)
    hbm = pl.BlockSpec(memory_space=pl.ANY)
    dma = pltpu.SemaphoreType.DMA
    out, loss = pl.pallas_call(
        kernel,
        out_shape=(jax.ShapeDtypeStruct((128, 2048), BF), jax.ShapeDtypeStruct((1, 1), F32)),
        in_specs=[vmem, vmem, vmem, hbm, hbm, hbm, hbm],
        out_specs=(vmem, vmem),
        scratch_shapes=[
            pltpu.VMEM((128, 2048), F32),
            pltpu.VMEM((8, 2, 4, 4, 128, 128), BF),
            pltpu.VMEM((16, 128), F32),
            pltpu.VMEM((16, 16, 128), F32),
            pltpu.VMEM((8, 256, 2048), BF),
            pltpu.VMEM((8, 256, 128), BF),
            pltpu.VMEM((8, 256, 2048), BF),
            pltpu.VMEM((8, 128, 2048), BF),
            pltpu.VMEM((16, 128, 128), BF),
            pltpu.VMEM((16, 128, 128), BF),
            pltpu.VMEM((8, 256, 128), F32),
            pltpu.VMEM((8, 4, 4, 128, 128), BF),
            pltpu.VMEM((8, 4, 4, 128, 128), BF),
            pltpu.VMEM((8, 4, 4, 128, 128), BF),
            pltpu.VMEM((8, 6, 2, 128, 128), BF),
            pltpu.VMEM((8, 3, 128, 128), BF),
            pltpu.VMEM((8, 2, 2, 128, 128), BF),
            pltpu.VMEM((8, 4, 128, 128), BF),
            pltpu.VMEM((8, 128, 128), F32),
            pltpu.VMEM((16, 128, 128), BF),
            pltpu.VMEM((2, 4, 4, 64, 128), BF),
            pltpu.VMEM((8, 128), F32),
            pltpu.VMEM((16, 8, 128), F32),
            pltpu.VMEM((2, 8, 128), F32),
            pltpu.VMEM((4, 8, 128), F32),
            pltpu.VMEM((4, 8, 128), F32),
            dma((4,)), dma((8,)), dma((8,)), dma((16,)), dma((16,)),
            dma((8, 3)), dma((8, 3)), dma((8, 6)), dma((8, 6)),
            dma((8,)), dma((8,)), dma((8,)), dma((8,)),
            dma((8, 6)), dma((8, 6)), dma((8, 3)), dma((8, 3)),
            dma((8,)), dma((8,)), dma((16,)), dma((16,)), dma((24,)), dma((24,)),
        ],
        compiler_params=pltpu.CompilerParams(
            collective_id=0, has_side_effects=True, vmem_limit_bytes=62 * 1024 * 1024),
    )(expert_ids.T, gate_values.T, valid_mask.reshape(1, 128), tokens, gate_weight, up_weight, down_weight)
    return out.astype(F32), loss.reshape(())


def solution(mesh):
    return jax.shard_map(
        on_device,
        mesh=mesh,
        in_specs=(
            P("expert", None),
            P("expert", None),
            P("expert", None),
            P("expert"),
            P("expert", "dp", None),
            P("expert", "dp", None),
            P("expert", "dp", None),
        ),
        out_specs=(P("expert", None), P()),
        check_vma=False,
    )
```

time: 416 us -> 105 us (0.25)
  waiting for transfers between devices: 240 us -> 0 us
  Pallas kernels: 0 us -> 100 us
  blocking collectives: 74.3 us -> 0 us
  matrix products: 42.7 us -> 0 us
  local copies, waits for them, and re-layouts: 29.2 us -> 0 us
  between operations: 16.3 us -> 2.34 us
  other arithmetic: 9.1 us -> 2.12 us
    pallas_call x0 -> x1, Pallas kernels: none -> 100 us  [on_device(): pl.pallas_call(kernel, out_shape=(jax.ShapeDtypeStruct((128, 2048), BF),...]
    all_gather x2 -> x0, waiting for transfers between devices: 94.6 us -> none  [the longest x1 51.8 us: on_device(): blended = lax.all_gather(own, 'dp', axis=1, tiled=True)]
    unnamed x5 -> x0, waiting for transfers between devices: 90.4 us -> none
    reduce_scatter x1 -> x0, waiting for transfers between devices: 54.8 us -> none  [on_device(): lax.psum_scatter(summed.astype(jnp.float32), 'expert', scatter_dimension=...]
    all_gather x3 -> x0, blocking collectives: 52 us -> none  [the longest x1 20.7 us: on_device(): column = lax.all_gather(mine, 'expert', axis=0, tiled=True)]
    dot_general x4 -> x0, matrix products: 42.7 us -> none  [the longest x1 15.4 us: on_device(): jnp.einsum('erf,efd->erd', hidden, down_weight, preferred_element_type=jn...]
    psum x1 -> x0, blocking collectives: 22.3 us -> none  [on_device(): loss_sum, token_total = lax.psum((local_loss, jnp.sum(weights)), 'expert')]
    unnamed x11 -> x0, local copies, waits for them, and re-layouts: 16.8 us -> none
  transfers between devices with their start and end apart: 4 -> 0, of which waited for: 4 -> 0; matrix products, arithmetic and copies ran while one was open for 2% -> 0% of each run, Pallas kernels for 0% -> 0%
where the time goes in v3:
time: 105 us; the launch traced here: 104 us
  Pallas kernels  100 us (95%)
  between operations  2.34 us (2%)
  other arithmetic  2.12 us (2%)
    pallas_call x1, Pallas kernels, on_device(): pl.pallas_call(kernel, out_shape=(jax.ShapeDtypeStruct((128, 2048), BF),...  100 us
    convert_element_type x1, other arithmetic, on_device(): return (out.astype(F32), loss.reshape(()))  2.12 us

profile of v3, /device:TPU:32, one launch (start us, length us, event | category | flops | bytes accessed | tf_op | source)
XLA Modules:
  0.0 104.5 jit_solution(14652478804859070213)
XLA Ops:
  0.6 100.0 %shard_map.86 = (bf16[128,2048]{1,0:T(8,128)(2,1)}, f32[1,1]{1,0:T(1,128)}) custom-call(s32[8,128]{1,0:T(8,128)} %bitcast.4, f32[8,128]{1,0:T(8,128)} %bitcast.5, s32[1,128]{1,0:T(1,128)} %bitcast.6, f32[128,2048]{1,0:T(8,128)} %tok.1, bf16[8,96,2048]{2,1,0:T(8,128)(2,1)} %gw.1, bf16[8,96,2048]{2,1,0:T(8,128)(2,1)} %uw.1, bf16[8,96,2048]{2,1,0:T(8,128)(2,1)} %dw.1), custom_call_target="tpu_custom_call" | custom-call | tf_op jit(solution)/shard_map/pallas_call | solution.py:419
  100.7 2.1 %convert_element_type.3 = f32[128,2048]{1,0:T(8,128)} convert(bf16[128,2048]{1,0:T(8,128)(2,1)} %get-tuple-element.4) | non-fusion elementwise | flops 262144 | bytes 1572864 | tf_op jit(solution)/shard_map/convert_element_type | solution.py:460

commit v4 on v3

--- a/solution.py
+++ b/solution.py
@@ -9,16 +9,17 @@
 BF = jnp.bfloat16
 F32 = jnp.float32
 SLOTS = 16
-ORDER = (0, 2, 6, 3, 5, 4, 1, 7)
+ORDER = (0, 2, 6, 4, 3, 5, 1, 7)
 POS = {dz: k for k, dz in enumerate(ORDER)}
-GZ, G0, G1 = (0,), (2, 6, 3, 5), (4, 1, 7)
-PLANE = (2, 6, 3, 5, 4)
-XFIRST = {0: False, 2: True, 6: False, 3: True, 5: False, 4: True, 1: False, 7: True}
+GROUPS = ((0,), (2,), (6, 4), (3, 5, 1, 7))
+PLANE = (2, 6, 4, 3, 5)
+(META_K, SLICE_K, WHOLE_K, A_K, B_K, P_K, Q_K, RB_K, RA_K, V_K, F1_K, F2_K, L_K, LX_K, LY_K) = range(15)
+XFIRST = {0: False, 2: True, 6: False, 4: True, 3: False, 5: True, 1: False, 7: True}
 
 
 def kernel(ids, gates, mask, tok, gw, uw, dw, out, loss,
            TOKF, TOK, MINE, META, X, H, W1, WD, SEL, STR, GS, PART, PX, PEX, RB, RA, ACCB, SUMB, Q, ZR, FIN, LS, LR, LT, LX, LY,
-           wsem, zs, zr, ms, mr, as_, ar, bs, br, ps, pr, qs, qr, rbs, rbr, ras, rar, vs, vr, fs, fr, ls, lr):
+           wsem, out_sem, zr, mr, ar, br, pr, qr, rbr, rar, vr, fr, lr):
     dp = lax.axis_index("dp")
     ex = lax.axis_index("expert")
     y, x = dp // 4, dp % 4
@@ -37,15 +38,14 @@
         return pltpu.make_async_remote_copy(
             src_ref=src, dst_ref=dst, send_sem=ssem, recv_sem=rsem, device_id=dev, device_id_type=MESH)
 
-    pending = []
-
-    def send(src, dst, ssem, rsem, dev):
-        cp = remote(src, dst, ssem, rsem, dev)
-        cp.start()
-        pending.append(cp)
-
-    def arrive(dst, ssem, rsem):
-        remote(dst, dst, ssem, rsem, peer(0, 1)).wait_recv()
+    def send(src, dst, kind, rsem, dev):
+        remote(src, dst, out_sem.at[kind], rsem, dev).start()
+
+    def arrive(dst, rsem):
+        remote(dst, dst, out_sem.at[0], rsem, peer(0, 1)).wait_recv()
+
+    def sent(kind, like):
+        remote(like, like, out_sem.at[kind], mr.at[0], peer(0, 1)).wait_send()
 
     load = pltpu.make_async_copy(tok, TOKF, wsem.at[3])
     load.start()
@@ -80,23 +80,23 @@
         return (8 - dz) % 8
 
     def meta(dz):
-        send(MINE, META.at[2 * POS[back(dz)]], ms.at[dz], mr.at[2 * POS[back(dz)]], peer(dz, 0))
+        send(MINE, META.at[2 * POS[back(dz)]], META_K, mr.at[2], peer(dz, 0))
 
     def slice_to(dz):
-        send(TOK.at[0, 0, y, x], TOK.at[back(dz), 0, y, x], zs.at[dz], zr.at[back(dz)], peer(dz, 0))
-
-    send(MINE, META.at[1], ms.at[0], mr.at[1], peer(0, 1))
-    slice_to(2)
-    slice_to(6)
-    send(TOK.at[0, 0], TOK.at[0, 1], ps.at[0], pr.at[0], peer(0, 1))
+        send(TOK.at[0, 0, y, x], TOK.at[back(dz), 0, y, x], SLICE_K, zr.at[back(dz)], peer(dz, 0))
+
+    send(MINE, META.at[1], META_K, mr.at[1], peer(0, 1))
+    for dz in PLANE[:2]:
+        slice_to(back(dz))
+    send(TOK.at[0, 0], TOK.at[0, 1], P_K, pr.at[0], peer(0, 1))
     for dz in PLANE[2:]:
-        slice_to(dz)
+        slice_to(back(dz))
     for dz in ORDER[1:]:
         meta(dz)
 
     def whole():
-        send(TOK.at[0, 0], TOK.at[7, 0], zs.at[1], zr.at[7], peer(1, 0))
-        send(TOK.at[0, 0], TOK.at[1, 0], zs.at[7], zr.at[1], peer(7, 0))
+        send(TOK.at[0, 0], TOK.at[7, 0], WHOLE_K, zr.at[7], peer(1, 0))
+        send(TOK.at[0, 0], TOK.at[1, 0], WHOLE_K, zr.at[1], peer(7, 0))
 
     zero = jnp.zeros((32, 2048), BF)
     for e in range(8):
@@ -119,32 +119,32 @@
 
     def t1(dz):
         a, b, ma, mb = near(dz)
-        arrive(TOK.at[dz, 0, y, x], zs.at[dz], zr.at[dz])
+        arrive(TOK.at[dz, 0, y, x], zr.at[dz])
         for d in (2, 1, 3):
-            send(piece(dz, ma), piece(dz, ma), as_.at[dz, d - 1], ar.at[dz, d - 1], step(a, d))
+            send(piece(dz, ma), piece(dz, ma), A_K, ar.at[PLANE.index(dz)], step(a, d))
 
     def t3(dz):
         a, b, ma, mb = near(dz)
-        for d in (1, 3, 2):
-            arrive(piece(dz, ma - d), as_.at[dz, d - 1], ar.at[dz, d - 1])
-        for n, h, d in ((0, 0, 1), (1, 1, -1), (2, 1, 1), (3, 0, -1)):
-            send(bundle_half(dz, mb, h), bundle_half(dz, mb, h), bs.at[dz, n], br.at[dz, n], step(b, d))
+        k = PLANE.index(dz)
+        arrive(RA.at[0], ar.at[k])
+        for n, h, d in ((0, 0, 1), (1, 1, -1), (2, 1, 1), (2, 0, -1)):
+            send(bundle_half(dz, mb, h), bundle_half(dz, mb, h), B_K, br.at[k, n], step(b, d))
 
     def t4(dz):
         a, b, ma, mb = near(dz)
+        k = PLANE.index(dz)
         for n, h, d in ((0, 0, 1), (1, 1, -1)):
             got = bundle_half(dz, mb - d, h)
-            arrive(got, bs.at[dz, n], br.at[dz, n])
-            send(got, got, bs.at[dz, 4 + n], br.at[dz, 4 + n], step(b, d))
+            arrive(got, br.at[k, n])
+            send(got, got, B_K, br.at[k, 2], step(b, d))
 
     def t5(dz):
         a, b, ma, mb = near(dz)
         if dz in PLANE:
-            for n, h, d in ((2, 1, 1), (3, 0, -1), (4, 0, 2), (5, 1, -2)):
-                arrive(bundle_half(dz, mb - d, h), bs.at[dz, n], br.at[dz, n])
+            arrive(RB.at[dz, pl.ds(2, 4)], br.at[PLANE.index(dz), 2])
         else:
-            arrive(TOK.at[dz, 0], zs.at[dz], zr.at[dz])
-        send(TOK.at[dz, 0], TOK.at[dz, 1], ps.at[dz], pr.at[dz], peer(0, 1))
+            arrive(TOK.at[dz, 0], zr.at[dz])
+        send(TOK.at[dz, 0], TOK.at[dz, 1], P_K, pr.at[dz], peer(0, 1))
 
     row = lax.broadcasted_iota(jnp.int32, (128, 128), 0)
     col = lax.broadcasted_iota(jnp.int32, (128, 128), 1)
@@ -171,24 +171,23 @@
             jnp.sum(held, axis=2, keepdims=True), (8, SLOTS, 128))
         return carry
 
-    def metas():
-        for dz in ORDER[1:]:
-            arrive(META.at[2 * POS[dz]], ms.at[dz], mr.at[2 * POS[dz]])
+    def metas1():
+        arrive(META.at[pl.ds(0, 7)], mr.at[2])
         for dz in ORDER[1:]:
             k = 2 * POS[dz]
-            send(META.at[k], META.at[k + 1], ms.at[8 + dz], mr.at[k + 1], peer(0, 1))
-        for dz in ORDER[1:]:
-            k = 2 * POS[dz]
-            arrive(META.at[k + 1], ms.at[8 + dz], mr.at[k + 1])
+            send(META.at[k], META.at[k + 1], META_K, mr.at[3], peer(0, 1))
+
+    def metas2():
+        arrive(META.at[pl.ds(0, 7)], mr.at[3])
         lax.fori_loop(2, 16, route, 0)
 
     def own_plane():
-        arrive(META.at[1], ms.at[0], mr.at[1])
+        arrive(META.at[1], mr.at[1])
         lax.fori_loop(0, 2, route, 0)
 
     def select(dz, rc):
         if rc:
-            arrive(TOK.at[dz, 1], ps.at[dz], pr.at[dz])
+            arrive(TOK.at[dz, 1], pr.at[dz])
         k = 2 * POS[dz] + rc
         pick = SEL[k]
         for i in range(4):
@@ -235,7 +234,7 @@
             got = combine(dz, 1, i).astype(BF)
             for j in range(4):
                 PX[dz, i, j] = got[:, j * 128:(j + 1) * 128]
-        send(PX.at[dz], PEX.at[dz], qs.at[dz], qr.at[dz], peer(0, 1))
+        send(PX.at[dz], PEX.at[dz], Q_K, qr.at[dz], peer(0, 1))
 
     def home(dz, pos, h):
         two = pl.ds(2 * h, 2)
@@ -249,167 +248,201 @@
 
     def r1(dz):
         a, b, ma, mb = near(dz)
-        arrive(PEX.at[dz], qs.at[dz], qr.at[dz])
+        arrive(PEX.at[dz], qr.at[dz])
         for i in range(4):
             got = combine(dz, 0, i)
             for j in range(4):
                 PART[dz, i, j] = (got[:, j * 128:(j + 1) * 128] + PEX[dz, i, j].astype(F32)).astype(BF)
-        send(home(dz, mb + 2, 0), RB.at[dz, 0], rbs.at[dz, 0], rbr.at[dz, 0], step(b, 1))
-        send(home(dz, mb + 2, 1), RB.at[dz, 1], rbs.at[dz, 1], rbr.at[dz, 1], step(b, -1))
-        send(home(dz, mb - 1, 0), RB.at[dz, 3], rbs.at[dz, 3], rbr.at[dz, 3], step(b, -1))
-        send(home(dz, mb + 1, 1), RB.at[dz, 4], rbs.at[dz, 4], rbr.at[dz, 4], step(b, 1))
+        for n, pos, h, d in ((0, 2, 0, 1), (1, 2, 1, -1), (3, -1, 0, -1), (4, 1, 1, 1)):
+            send(home(dz, mb + pos, h), RB.at[dz, n], RB_K, rbr.at[dz, min(n, 2)], step(b, d))
 
     def r2(dz):
         a, b, ma, mb = near(dz)
         for n, d in ((0, 1), (1, -1)):
-            arrive(RB.at[dz, n], rbs.at[dz, n], rbr.at[dz, n])
+            arrive(RB.at[dz, n], rbr.at[dz, n])
             ACCB[dz, n] = plus(RB.at[dz, n], home(dz, mb + d, n)).astype(BF)
         for n, d, m in ((0, 1, 2), (1, -1, 5)):
-            send(ACCB.at[dz, n], RB.at[dz, m], rbs.at[dz, m], rbr.at[dz, m], step(b, d))
+            send(ACCB.at[dz, n], RB.at[dz, m], RB_K, rbr.at[dz, 2], step(b, d))
 
     def r3(dz):
         a, b, ma, mb = near(dz)
-        for n in (3, 4, 2, 5):
-            arrive(RB.at[dz, n], rbs.at[dz, n], rbr.at[dz, n])
+        arrive(RB.at[dz, pl.ds(2, 4)], rbr.at[dz, 2])
         SUMB[dz, 0:2] = plus(home(dz, mb, 0), RB.at[dz, 2], RB.at[dz, 3]).astype(BF)
         SUMB[dz, 2:4] = plus(home(dz, mb, 1), RB.at[dz, 4], RB.at[dz, 5]).astype(BF)
         for d in (2, 1, 3):
-            send(SUMB.at[dz, wrap(ma + d)], RA.at[dz, d - 1], ras.at[dz, d - 1], rar.at[dz, d - 1], step(a, d))
+            send(SUMB.at[dz, wrap(ma + d)], RA.at[dz, d - 1], RA_K, rar.at[dz], step(a, d))
 
     def r5(dz):
         a, b, ma, mb = near(dz)
-        for d in (1, 3, 2):
-            arrive(RA.at[dz, d - 1], ras.at[dz, d - 1], rar.at[dz, d - 1])
+        arrive(RA.at[dz], rar.at[dz])
         Q[dz] = plus(SUMB.at[dz, ma], RA.at[dz, 0], RA.at[dz, 1], RA.at[dz, 2])
         if dz:
             ZR[8 + dz] = Q[dz].astype(BF)
-            send(ZR.at[8 + dz], ZR.at[back(dz)], vs.at[dz], vr.at[back(dz)], peer(dz, 0))
+            send(ZR.at[8 + dz], ZR.at[back(dz)], V_K, vr.at[0], peer(dz, 0))
 
     def each(task, group):
         for dz in group:
             task(dz)
 
-
     own_plane()
     select(0, 0)
-    each(t1, (2, 6))
     select(0, 1)
     for w in weights:
         w.wait()
-    ups(GZ, 0, 4)
-    each(t1, (3, 5))
-    each(t3, (2, 6))
-    ups(GZ, 4, 8)
+    ups(GROUPS[0], 0, 4)
+    t1(6)
+    t1(2)
+    ups(GROUPS[0], 4, 8)
+    downs(GROUPS[0], 0, 4)
+    downs(GROUPS[0], 4, 8)
+    t3(6)
+    t3(2)
     t1(4)
+    give(0)
+    t1(3)
+    t1(5)
     whole()
-    each(t4, (2, 6))
-    each(t3, (3, 5))
-    downs(GZ, 0, 8)
-    give(0)
-    metas()
-    each(t5, (2, 6))
-    each(t4, (3, 5))
+    r1(0)
+    metas1()
+    t4(2)
+    t4(6)
+    metas2()
+    t3(3)
     t3(4)
-    r1(0)
+    t3(5)
+    t5(2)
     select(2, 0)
+    r2(0)
+    t4(4)
+    select(2, 1)
+    ups(GROUPS[1], 0, 4)
+    ups(GROUPS[1], 4, 8)
+    t5(6)
+    t4(5)
+    downs(GROUPS[1], 0, 4)
+    t4(3)
+    downs(GROUPS[1], 4, 8)
+    give(2)
     select(6, 0)
-    each(t5, (3, 5))
-    select(2, 1)
     select(6, 1)
-    t4(4)
-    r2(0)
+    t5(4)
+    select(4, 0)
+    t5(1)
+    select(1, 0)
+    r3(0)
+    r1(2)
+    t5(5)
+    select(5, 0)
+    t5(7)
+    select(7, 0)
+    select(4, 1)
+    t5(3)
     select(3, 0)
-    select(5, 0)
+    ups(GROUPS[2], 0, 4)
+    r5(0)
+    ups(GROUPS[2], 4, 8)
+    downs(GROUPS[2], 0, 4)
+    select(5, 1)
+    downs(GROUPS[2], 4, 8)
+    give(6)
     select(3, 1)
-    select(5, 1)
-    ups(G0, 0, 4)
-    t5(4)
-    r3(0)
-    ups(G0, 4, 8)
-    downs(G0, 0, 8)
-    each(give, G0)
-    each(t5, (1, 7))
-    select(4, 0)
-    select(4, 1)
-    select(1, 0)
-    select(7, 0)
-    each(r1, G0)
+    give(4)
     select(1, 1)
+    r2(2)
     select(7, 1)
-    r5(0)
-    ups(G1, 0, 4)
-    each(r2, G0)
-    ups(G1, 4, 8)
-    downs(G1, 0, 4)
-    each(r3, G0)
-    downs(G1, 4, 8)
-    each(give, G1)
-    each(r5, G0)
-    each(r1, G1)
-    each(r2, G1)
-    each(r3, G1)
-    each(r5, G1)
+    ups(GROUPS[3], 0, 4)
+    r1(6)
+    r1(4)
+    ups(GROUPS[3], 4, 8)
+    downs(GROUPS[3], 0, 4)
+    r2(6)
+    downs(GROUPS[3], 4, 8)
+    give(3)
+    give(5)
+    r2(4)
+    give(7)
+    r3(2)
+    give(1)
+    r3(6)
+    r1(3)
+    r1(5)
+    r5(2)
+    r3(4)
+    r1(7)
+    r5(6)
+    r2(3)
+    r1(1)
+    r2(5)
+    r5(4)
+    r3(3)
+    r2(7)
+    r2(1)
+    r3(5)
+    r5(3)
+    r3(1)
+    r3(7)
+    r5(5)
+    r5(1)
+    r5(7)
+    arrive(ZR.at[pl.ds(1, 7)], vr.at[0])
     total = Q[0]
     for dz in ORDER[1:]:
-        arrive(ZR.at[dz], vs.at[dz], vr.at[dz])
         total = total + ZR[dz].astype(F32)
     FIN[0, y, x] = total[0:64].astype(BF)
     FIN[1, y, x] = total[64:128].astype(BF)
+    LS[...] = jnp.sum((total * total).reshape(16, 8, 128), axis=0)
 
     def strip(h, first, pos):
         if first:
             return FIN.at[0, y, wrap(pos)] if h == 0 else FIN.at[1, wrap(pos), x]
         return FIN.at[0, wrap(pos)] if h == 0 else FIN.at[1, :, wrap(pos)]
 
-    for first in (True, False):
-        base = 0 if first else 8
+    def gather(first):
         legs = (("x", x), ("y", y)) if first else (("y", y), ("x", x))
-        for d in (1, 3, 2):
+        for d in (2, 1, 3):
             for h, (axis, me) in enumerate(legs):
-                n = base + 4 * h + d
-                send(strip(h, first, me), strip(h, first, me), fs.at[n], fr.at[n], step(axis, d))
-        if first:
-            LS[...] = jnp.sum((total * total).reshape(16, 8, 128), axis=0)
-            for dz in ORDER:
-                for rc in range(2):
-                    if (dz, rc) != (0, 0):
-                        k, kb = 2 * POS[dz] + rc, 2 * POS[back(dz)] + rc
-                        send(LS, LR.at[kb], ls.at[k], lr.at[kb], peer(dz, rc))
-            LR[0] = LS[...]
-        for d in (1, 3, 2):
-            for h, (axis, me) in enumerate(legs):
-                n = base + 4 * h + d
-                arrive(strip(h, first, me - d), fs.at[n], fr.at[n])
-        if first:
-            continue
-
-    for k in range(1, 16):
-        arrive(LR.at[k], ls.at[k], lr.at[k])
+                send(strip(h, first, me), strip(h, first, me), F1_K if first else F2_K,
+                     fr.at[0 if first else 1], step(axis, d))
+
+    gather(True)
+    for dz in (4, 3, 5, 2, 6, 1, 7, 0):
+        for rc in range(2):
+            if (dz, rc) != (0, 0):
+                send(LS, LR.at[2 * POS[back(dz)] + rc], L_K, lr.at[0], peer(dz, rc))
+    LR[0] = LS[...]
+    count = jnp.sum(jnp.where(META[...][:, 0:1, :] >= 0.0, 1.0, 0.0), axis=0)
+    count = jnp.sum(count, axis=1, keepdims=True)
+    arrive(RA.at[0], fr.at[0])
+    gather(False)
+
+    arrive(LR.at[pl.ds(1, 15)], lr.at[0])
     LT[0] = jnp.sum(LR[...], axis=0)
-    for d in (1, 3, 2):
-        send(LT.at[0], LX.at[d], ls.at[16 + d], lr.at[16 + d], step("x", d))
+    LX[0] = LT[0]
+    for d in (2, 1, 3):
+        send(LT.at[0], LX.at[d], LX_K, lr.at[1], step("x", d))
+    arrive(LX.at[pl.ds(1, 3)], lr.at[1])
+    LT[1] = jnp.sum(LX[...], axis=0)
+    LY[0] = LT[1]
+    for d in (2, 1, 3):
+        send(LT.at[1], LY.at[d], LY_K, lr.at[2], step("y", d))
+    arrive(RB.at[0], fr.at[1])
     for i in range(4):
         for j in range(4):
             f = (i * 4 + j) * 128
             out[0:64, f:f + 128] = FIN[0, i, j].astype(out.dtype)
             out[64:128, f:f + 128] = FIN[1, i, j].astype(out.dtype)
-    LX[0] = LT[0]
-    for d in (1, 3, 2):
-        arrive(LX.at[d], ls.at[16 + d], lr.at[16 + d])
-    LT[1] = jnp.sum(LX[...], axis=0)
-    for d in (1, 3, 2):
-        send(LT.at[1], LY.at[d], ls.at[20 + d], lr.at[20 + d], step("y", d))
-    count = jnp.sum(jnp.where(META[...][:, 0:1, :] >= 0.0, 1.0, 0.0), axis=0)
-    count = jnp.sum(count, axis=1, keepdims=True)
-    LY[0] = LT[1]
-    for d in (1, 3, 2):
-        arrive(LY.at[d], ls.at[20 + d], lr.at[20 + d])
+    arrive(LY.at[pl.ds(1, 3)], lr.at[2])
     top = jnp.sum(LY[...], axis=0)
     top = jnp.sum(jnp.sum(top, axis=0, keepdims=True), axis=1, keepdims=True) * (1.0 / 2048.0)
     loss[...] = top / count
 
-    for cp in pending:
-        cp.wait_send()
+    for kind, like in (
+        (META_K, META.at[pl.ds(1, 15)]), (SLICE_K, ZR.at[pl.ds(0, 5)]), (WHOLE_K, PX.at[pl.ds(0, 2)]),
+        (A_K, RA.at[pl.ds(0, 5)]), (B_K, RB.at[pl.ds(0, 5)]), (P_K, PX), (Q_K, PX), (RB_K, RB), (RA_K, RA),
+        (V_K, ZR.at[pl.ds(1, 7)]), (F1_K, RA.at[0]), (F2_K, RB.at[0]), (L_K, LR.at[pl.ds(1, 15)]),
+        (LX_K, LX.at[pl.ds(1, 3)]), (LY_K, LY.at[pl.ds(1, 3)]),
+    ):
+        sent(kind, like)
 
 
 def on_device(tokens, expert_ids, gate_values, valid_mask, gate_weight, up_weight, down_weight):
@@ -448,11 +481,8 @@
             pltpu.VMEM((2, 8, 128), F32),
             pltpu.VMEM((4, 8, 128), F32),
             pltpu.VMEM((4, 8, 128), F32),
-            dma((4,)), dma((8,)), dma((8,)), dma((16,)), dma((16,)),
-            dma((8, 3)), dma((8, 3)), dma((8, 6)), dma((8, 6)),
-            dma((8,)), dma((8,)), dma((8,)), dma((8,)),
-            dma((8, 6)), dma((8, 6)), dma((8, 3)), dma((8, 3)),
-            dma((8,)), dma((8,)), dma((16,)), dma((16,)), dma((24,)), dma((24,)),
+            dma((4,)), dma((15,)), dma((8,)), dma((4,)), dma((5,)), dma((5, 3)), dma((8,)), dma((8,)),
+            dma((8, 3)), dma((8,)), dma((1,)), dma((2,)), dma((3,)),
         ],
         compiler_params=pltpu.CompilerParams(
             collective_id=0, has_side_effects=True, vmem_limit_bytes=62 * 1024 * 1024),

time: 105 us -> 96 us (0.914)
  Pallas kernels: 100 us -> 91.3 us
    pallas_call x1, Pallas kernels: 100 us -> 91.3 us  [on_device(): pl.pallas_call(kernel, out_shape=(jax.ShapeDtypeStruct((128, 2048), BF),...]
where the time goes in v4:
time: 96 us; the launch traced here: 95.7 us
  Pallas kernels  91.3 us (95%)
  between operations  2.34 us (2%)
  other arithmetic  2.12 us (2%)
    pallas_call x1, Pallas kernels, on_device(): pl.pallas_call(kernel, out_shape=(jax.ShapeDtypeStruct((128, 2048), BF),...  91.3 us
    convert_element_type x1, other arithmetic, on_device(): return (out.astype(F32), loss.reshape(()))  2.12 us

profile of v4, /device:TPU:32, one launch (start us, length us, event | category | flops | bytes accessed | tf_op | source)
XLA Modules:
  0.0 95.7 jit_solution(12925242651925496897)
XLA Ops:
  0.6 91.3 %shard_map.86 = (bf16[128,2048]{1,0:T(8,128)(2,1)}, f32[1,1]{1,0:T(1,128)}) custom-call(s32[8,128]{1,0:T(8,128)} %bitcast.4, f32[8,128]{1,0:T(8,128)} %bitcast.5, s32[1,128]{1,0:T(1,128)} %bitcast.6, f32[128,2048]{1,0:T(8,128)} %tok.1, bf16[8,96,2048]{2,1,0:T(8,128)(2,1)} %gw.1, bf16[8,96,2048]{2,1,0:T(8,128)(2,1)} %uw.1, bf16[8,96,2048]{2,1,0:T(8,128)(2,1)} %dw.1), custom_call_target="tpu_custom_call" | custom-call | tf_op jit(solution)/shard_map/pallas_call | solution.py:452
  91.9 2.1 %convert_element_type.3 = f32[128,2048]{1,0:T(8,128)} convert(bf16[128,2048]{1,0:T(8,128)(2,1)} %get-tuple-element.4) | non-fusion elementwise | flops 262144 | bytes 1572864 | tf_op jit(solution)/shard_map/convert_element_type | solution.py:490

commit v5 on v4

--- a/solution.py
+++ b/solution.py
@@ -9,16 +9,17 @@
 BF = jnp.bfloat16
 F32 = jnp.float32
 SLOTS = 16
-ORDER = (0, 2, 6, 4, 3, 5, 1, 7)
+ORDER = (0, 2, 6, 3, 5, 4, 1, 7)
 POS = {dz: k for k, dz in enumerate(ORDER)}
-GROUPS = ((0,), (2,), (6, 4), (3, 5, 1, 7))
-PLANE = (2, 6, 4, 3, 5)
-(META_K, SLICE_K, WHOLE_K, A_K, B_K, P_K, Q_K, RB_K, RA_K, V_K, F1_K, F2_K, L_K, LX_K, LY_K) = range(15)
-XFIRST = {0: False, 2: True, 6: False, 4: True, 3: False, 5: True, 1: False, 7: True}
+GROUPS = ((0,), (2, 6, 3), (5, 4, 1, 7))
+PLANE = (2, 6, 3, 5, 4)
+FAST_OUT, FAST_IN = (6,), ()
+(META_K, SLICE_K, WHOLE_K, A_K, B_K, P_K, Q_K, RB_K, RA_K, V_K, F1_K, F2_K, L_K, LX_K) = range(14)
+XFIRST = {0: False, 2: True, 6: False, 3: True, 5: False, 4: True, 1: False, 7: True}
 
 
 def kernel(ids, gates, mask, tok, gw, uw, dw, out, loss,
-           TOKF, TOK, MINE, META, X, H, W1, WD, SEL, STR, GS, PART, PX, PEX, RB, RA, ACCB, SUMB, Q, ZR, FIN, LS, LR, LT, LX, LY,
+           TOKF, TOK, MINE, META, X, H, W1, WD, SEL, STR, GS, PART, PX, PEX, RB, RA, ACCB, SUMB, Q, ZR, FIN, LS, LR, LT, LX,
            wsem, out_sem, zr, mr, ar, br, pr, qr, rbr, rar, vr, fr, lr):
     dp = lax.axis_index("dp")
     ex = lax.axis_index("expert")
@@ -34,6 +35,9 @@
             return {"dp": y * 4 + (x + d + 4) % 4, "expert": ex}
         return {"dp": ((y + d + 4) % 4) * 4 + x, "expert": ex}
 
+    def across(i, j):
+        return {"dp": ((y + i) % 4) * 4 + (x + j) % 4, "expert": ex}
+
     def remote(src, dst, ssem, rsem, dev):
         return pltpu.make_async_remote_copy(
             src_ref=src, dst_ref=dst, send_sem=ssem, recv_sem=rsem, device_id=dev, device_id_type=MESH)
@@ -52,7 +56,7 @@
 
     barrier = pltpu.get_barrier_semaphore()
     everyone = [peer(dz, rc) for dz in range(8) for rc in range(2) if (dz, rc) != (0, 0)]
-    everyone += [step(axis, d) for axis in "xy" for d in (1, 2, 3)]
+    everyone += [across(i, j) for i in range(4) for j in range(4) if (i, j) != (0, 0)]
     for dev in everyone:
         pl.semaphore_signal(barrier, inc=1, device_id=dev, device_id_type=MESH)
 
@@ -127,12 +131,19 @@
         a, b, ma, mb = near(dz)
         k = PLANE.index(dz)
         arrive(RA.at[0], ar.at[k])
+        if dz in FAST_OUT:
+            for d in (2, 1, 3):
+                for h in range(2):
+                    send(bundle_half(dz, mb, h), bundle_half(dz, mb, h), B_K, br.at[k, 2], step(b, d))
+            return
         for n, h, d in ((0, 0, 1), (1, 1, -1), (2, 1, 1), (2, 0, -1)):
             send(bundle_half(dz, mb, h), bundle_half(dz, mb, h), B_K, br.at[k, n], step(b, d))
 
     def t4(dz):
         a, b, ma, mb = near(dz)
         k = PLANE.index(dz)
+        if dz in FAST_OUT:
+            return
         for n, h, d in ((0, 0, 1), (1, 1, -1)):
             got = bundle_half(dz, mb - d, h)
             arrive(got, br.at[k, n])
@@ -141,7 +152,7 @@
     def t5(dz):
         a, b, ma, mb = near(dz)
         if dz in PLANE:
-            arrive(RB.at[dz, pl.ds(2, 4)], br.at[PLANE.index(dz), 2])
+            arrive(RB.at[dz] if dz in FAST_OUT else RB.at[dz, pl.ds(2, 4)], br.at[PLANE.index(dz), 2])
         else:
             arrive(TOK.at[dz, 0], zr.at[dz])
         send(TOK.at[dz, 0], TOK.at[dz, 1], P_K, pr.at[dz], peer(0, 1))
@@ -253,11 +264,18 @@
             got = combine(dz, 0, i)
             for j in range(4):
                 PART[dz, i, j] = (got[:, j * 128:(j + 1) * 128] + PEX[dz, i, j].astype(F32)).astype(BF)
+        if dz in FAST_IN:
+            for d in (2, 1, 3):
+                for h in range(2):
+                    send(home(dz, mb + d, h), RB.at[dz, 2 * d - 2 + h], RB_K, rbr.at[dz, 2], step(b, d))
+            return
         for n, pos, h, d in ((0, 2, 0, 1), (1, 2, 1, -1), (3, -1, 0, -1), (4, 1, 1, 1)):
             send(home(dz, mb + pos, h), RB.at[dz, n], RB_K, rbr.at[dz, min(n, 2)], step(b, d))
 
     def r2(dz):
         a, b, ma, mb = near(dz)
+        if dz in FAST_IN:
+            return
         for n, d in ((0, 1), (1, -1)):
             arrive(RB.at[dz, n], rbr.at[dz, n])
             ACCB[dz, n] = plus(RB.at[dz, n], home(dz, mb + d, n)).astype(BF)
@@ -266,9 +284,10 @@
 
     def r3(dz):
         a, b, ma, mb = near(dz)
-        arrive(RB.at[dz, pl.ds(2, 4)], rbr.at[dz, 2])
-        SUMB[dz, 0:2] = plus(home(dz, mb, 0), RB.at[dz, 2], RB.at[dz, 3]).astype(BF)
-        SUMB[dz, 2:4] = plus(home(dz, mb, 1), RB.at[dz, 4], RB.at[dz, 5]).astype(BF)
+        arrive(RB.at[dz] if dz in FAST_IN else RB.at[dz, pl.ds(2, 4)], rbr.at[dz, 2])
+        low, high = ((0, 2, 4), (1, 3, 5)) if dz in FAST_IN else ((2, 3), (4, 5))
+        SUMB[dz, 0:2] = plus(home(dz, mb, 0), *[RB.at[dz, n] for n in low]).astype(BF)
+        SUMB[dz, 2:4] = plus(home(dz, mb, 1), *[RB.at[dz, n] for n in high]).astype(BF)
         for d in (2, 1, 3):
             send(SUMB.at[dz, wrap(ma + d)], RA.at[dz, d - 1], RA_K, rar.at[dz], step(a, d))
 
@@ -290,98 +309,94 @@
     for w in weights:
         w.wait()
     ups(GROUPS[0], 0, 4)
+    ups(GROUPS[0], 4, 8)
+    t1(2)
     t1(6)
-    t1(2)
-    ups(GROUPS[0], 4, 8)
     downs(GROUPS[0], 0, 4)
     downs(GROUPS[0], 4, 8)
-    t3(6)
-    t3(2)
-    t1(4)
     give(0)
     t1(3)
     t1(5)
+    t3(2)
+    t3(6)
+    t4(6)
+    r1(0)
+    t1(4)
     whole()
-    r1(0)
+    t3(3)
+    t3(5)
     metas1()
+    metas2()
     t4(2)
-    t4(6)
-    metas2()
-    t3(3)
-    t3(4)
-    t3(5)
+    t5(6)
+    select(6, 0)
+    t4(3)
+    r2(0)
+    select(6, 1)
     t5(2)
     select(2, 0)
-    r2(0)
+    t3(4)
+    t5(3)
+    select(3, 0)
+    select(2, 1)
+    t4(5)
+    select(3, 1)
+    ups(GROUPS[1], 0, 4)
+    t5(1)
+    t5(7)
     t4(4)
-    select(2, 1)
-    ups(GROUPS[1], 0, 4)
     ups(GROUPS[1], 4, 8)
-    t5(6)
-    t4(5)
+    t5(5)
     downs(GROUPS[1], 0, 4)
-    t4(3)
     downs(GROUPS[1], 4, 8)
     give(2)
-    select(6, 0)
-    select(6, 1)
+    select(7, 1)
     t5(4)
     select(4, 0)
-    t5(1)
+    select(5, 0)
+    give(3)
+    select(5, 1)
+    select(1, 1)
+    r3(0)
+    give(6)
+    select(7, 0)
+    r1(2)
     select(1, 0)
-    r3(0)
-    r1(2)
-    t5(5)
-    select(5, 0)
-    t5(7)
-    select(7, 0)
     select(4, 1)
-    t5(3)
-    select(3, 0)
     ups(GROUPS[2], 0, 4)
+    r1(3)
+    r1(6)
+    ups(GROUPS[2], 4, 8)
+    r2(2)
+    downs(GROUPS[2], 0, 4)
+    downs(GROUPS[2], 4, 8)
+    r2(6)
+    give(5)
+    give(4)
+    give(7)
+    give(1)
+    r2(3)
     r5(0)
-    ups(GROUPS[2], 4, 8)
-    downs(GROUPS[2], 0, 4)
-    select(5, 1)
-    downs(GROUPS[2], 4, 8)
-    give(6)
-    select(3, 1)
-    give(4)
-    select(1, 1)
-    r2(2)
-    select(7, 1)
-    ups(GROUPS[3], 0, 4)
-    r1(6)
+    r3(2)
+    r1(5)
+    r3(6)
     r1(4)
-    ups(GROUPS[3], 4, 8)
-    downs(GROUPS[3], 0, 4)
-    r2(6)
-    downs(GROUPS[3], 4, 8)
-    give(3)
-    give(5)
-    r2(4)
-    give(7)
-    r3(2)
-    give(1)
-    r3(6)
-    r1(3)
-    r1(5)
+    r1(7)
+    r3(3)
     r5(2)
-    r3(4)
-    r1(7)
-    r5(6)
-    r2(3)
     r1(1)
     r2(5)
-    r5(4)
-    r3(3)
+    r5(6)
+    r2(4)
+    r5(3)
+    r2(1)
     r2(7)
-    r2(1)
     r3(5)
-    r5(3)
+    r3(4)
     r3(1)
     r3(7)
     r5(5)
+    r5(4)
     r5(1)
     r5(7)
     arrive(ZR.at[pl.ds(1, 7)], vr.at[0])
@@ -408,8 +423,8 @@
     for dz in (4, 3, 5, 2, 6, 1, 7, 0):
         for rc in range(2):
             if (dz, rc) != (0, 0):
-                send(LS, LR.at[2 * POS[back(dz)] + rc], L_K, lr.at[0], peer(dz, rc))
-    LR[0] = LS[...]
+                send(LS, LR.at[ex], L_K, lr.at[0], peer(dz, rc))
+    LR[ex] = LS[...]
     count = jnp.sum(jnp.where(META[...][:, 0:1, :] >= 0.0, 1.0, 0.0), axis=0)
     count = jnp.sum(count, axis=1, keepdims=True)
     arrive(RA.at[0], fr.at[0])
@@ -417,22 +432,19 @@
 
     arrive(LR.at[pl.ds(1, 15)], lr.at[0])
     LT[0] = jnp.sum(LR[...], axis=0)
-    LX[0] = LT[0]
-    for d in (2, 1, 3):
-        send(LT.at[0], LX.at[d], LX_K, lr.at[1], step("x", d))
-    arrive(LX.at[pl.ds(1, 3)], lr.at[1])
-    LT[1] = jnp.sum(LX[...], axis=0)
-    LY[0] = LT[1]
-    for d in (2, 1, 3):
-        send(LT.at[1], LY.at[d], LY_K, lr.at[2], step("y", d))
+    LX[dp] = LT[0]
+    for i in range(4):
+        for j in range(4):
+            if (i, j) != (0, 0):
+                send(LT.at[0], LX.at[dp], LX_K, lr.at[1], across(i, j))
     arrive(RB.at[0], fr.at[1])
     for i in range(4):
         for j in range(4):
             f = (i * 4 + j) * 128
             out[0:64, f:f + 128] = FIN[0, i, j].astype(out.dtype)
             out[64:128, f:f + 128] = FIN[1, i, j].astype(out.dtype)
-    arrive(LY.at[pl.ds(1, 3)], lr.at[2])
-    top = jnp.sum(LY[...], axis=0)
+    arrive(LX.at[pl.ds(1, 15)], lr.at[1])
+    top = jnp.sum(LX[...], axis=0)
     top = jnp.sum(jnp.sum(top, axis=0, keepdims=True), axis=1, keepdims=True) * (1.0 / 2048.0)
     loss[...] = top / count
 
@@ -440,7 +452,7 @@
         (META_K, META.at[pl.ds(1, 15)]), (SLICE_K, ZR.at[pl.ds(0, 5)]), (WHOLE_K, PX.at[pl.ds(0, 2)]),
         (A_K, RA.at[pl.ds(0, 5)]), (B_K, RB.at[pl.ds(0, 5)]), (P_K, PX), (Q_K, PX), (RB_K, RB), (RA_K, RA),
         (V_K, ZR.at[pl.ds(1, 7)]), (F1_K, RA.at[0]), (F2_K, RB.at[0]), (L_K, LR.at[pl.ds(1, 15)]),
-        (LX_K, LX.at[pl.ds(1, 3)]), (LY_K, LY.at[pl.ds(1, 3)]),
+        (LX_K, LX.at[pl.ds(1, 15)]),
     ):
         sent(kind, like)
 
@@ -478,11 +490,10 @@
             pltpu.VMEM((2, 4, 4, 64, 128), BF),
             pltpu.VMEM((8, 128), F32),
             pltpu.VMEM((16, 8, 128), F32),
-            pltpu.VMEM((2, 8, 128), F32),
-            pltpu.VMEM((4, 8, 128), F32),
-            pltpu.VMEM((4, 8, 128), F32),
-            dma((4,)), dma((15,)), dma((8,)), dma((4,)), dma((5,)), dma((5, 3)), dma((8,)), dma((8,)),
-            dma((8, 3)), dma((8,)), dma((1,)), dma((2,)), dma((3,)),
+            pltpu.VMEM((1, 8, 128), F32),
+            pltpu.VMEM((16, 8, 128), F32),
+            dma((4,)), dma((14,)), dma((8,)), dma((4,)), dma((5,)), dma((5, 3)), dma((8,)), dma((8,)),
+            dma((8, 3)), dma((8,)), dma((1,)), dma((2,)), dma((2,)),
         ],
         compiler_params=pltpu.CompilerParams(
             collective_id=0, has_side_effects=True, vmem_limit_bytes=62 * 1024 * 1024),

time: 96 us -> 92.1 us (0.959)
  Pallas kernels: 91.3 us -> 86.6 us
    pallas_call x1, Pallas kernels: 91.3 us -> 86.6 us  [on_device(): pl.pallas_call(kernel, out_shape=(jax.ShapeDtypeStruct((128, 2048), BF),...]
where the time goes in v5:
time: 92.1 us; the launch traced here: 91 us
  Pallas kernels  86.6 us (94%)
  between operations  2.34 us (3%)
  other arithmetic  2.12 us (2%)
    pallas_call x1, Pallas kernels, on_device(): pl.pallas_call(kernel, out_shape=(jax.ShapeDtypeStruct((128, 2048), BF),...  86.6 us
    convert_element_type x1, other arithmetic, on_device(): return (out.astype(F32), loss.reshape(()))  2.12 us

profile of v5, /device:TPU:32, one launch (start us, length us, event | category | flops | bytes accessed | tf_op | source)
XLA Modules:
  0.0 91.0 jit_solution(3404668804405728299)
XLA Ops:
  0.6 86.6 %shard_map.86 = (bf16[128,2048]{1,0:T(8,128)(2,1)}, f32[1,1]{1,0:T(1,128)}) custom-call(s32[8,128]{1,0:T(8,128)} %bitcast.4, f32[8,128]{1,0:T(8,128)} %bitcast.5, s32[1,128]{1,0:T(1,128)} %bitcast.6, f32[128,2048]{1,0:T(8,128)} %tok.1, bf16[8,96,2048]{2,1,0:T(8,128)(2,1)} %gw.1, bf16[8,96,2048]{2,1,0:T(8,128)(2,1)} %uw.1, bf16[8,96,2048]{2,1,0:T(8,128)(2,1)} %dw.1), custom_call_target="tpu_custom_call" | custom-call | tf_op jit(solution)/shard_map/pallas_call | solution.py:464
  87.2 2.1 %convert_element_type.3 = f32[128,2048]{1,0:T(8,128)} convert(bf16[128,2048]{1,0:T(8,128)(2,1)} %get-tuple-element.4) | non-fusion elementwise | flops 262144 | bytes 1572864 | tf_op jit(solution)/shard_map/convert_element_type | solution.py:501
